TPU v7x, 128 devices: a whole 4x4x4 slice. The times are simulated.
128 devices in a mesh: tm: 32 (over x, y, core), chan: 4 (over z).
Axes of the slice: x: 4, y: 4, z: 4, core: 2. Of those that a mesh axis runs over, the one named last changes fastest.
Arguments:
- samples: float32 [64, 1048576], P('chan', 'tm'), may hold values from -6 to 6
- start_basis: float32 [512, 128], replicated, may hold values from -6 to 6
Outputs:
- factor: float32 [1024, 1024], P(('tm', 'chan'))
- states: float32 [128, 1048576], P(None, ('tm', 'chan'))
All inputs are finite; a program needn't handle non-finite values.
Results may differ from a plain program's by a relative error of at most 0.0003.
Values sent between devices are 32-bit elements; how exact they have to be, the bound alone decides.
No kernel may reach another device: no remote copies, remote signals or barrier semaphores. Data moves between devices by JAX's collectives and lax.ppermute only.
A program may use at most 256 MiB of HBM per device.

v0:
```python
import jax
import jax.numpy as jnp
from jax import lax
from jax.sharding import PartitionSpec as P

BR = 16
NSTEPS = 6


def from_behind(array, axis, by):
    size = lax.axis_size(axis)
    pairs = [(i, i + by) for i in range(size) if 0 <= i + by < size]
    return lax.ppermute(array, axis, pairs)


def upper_factor(gram):
    return jnp.linalg.cholesky(gram).T


def outer_gram(left, right):
    return lax.dot_general(
        left,
        right,
        (((1,), (1,)), ((), ())),
        precision=lax.Precision.HIGHEST,
        preferred_element_type=jnp.float32,
    )


def per_device(samples, start_basis):
    local = lax.all_to_all(samples, "chan", split_axis=1, concat_axis=0, tiled=True)
    count = local.shape[1]
    following = from_behind(local[:, : BR - 1], ("tm", "chan"), -1)
    extended = jnp.concatenate([local, following], 1)
    hankel = jnp.concatenate([extended[:, k : k + count] for k in range(BR)], 0)
    order = hankel.shape[0]
    half = order // 2
    total = count * lax.axis_size("tm") * lax.axis_size("chan")
    weight = 1.0 / (1.0 + jnp.mean(local * local, 0))
    gram = outer_gram(hankel * weight[None, :], hankel) * (1.0 / total)
    gram = lax.psum(gram, ("tm", "chan"))
    factor = upper_factor(gram)
    lead = jnp.dot(
        factor[half:, half:].T,
        start_basis,
        precision=lax.Precision.HIGHEST,
        preferred_element_type=jnp.float32,
    )
    basis = lead / jnp.sqrt(jnp.sum(lead * lead))
    for step in range(NSTEPS):
        inner = jnp.dot(
            basis.T, basis, precision=lax.Precision.HIGHEST, preferred_element_type=jnp.float32
        )
        basis = 1.5 * basis - 0.5 * jnp.dot(
            basis, inner, precision=lax.Precision.HIGHEST, preferred_element_type=jnp.float32
        )
    states = jnp.dot(
        basis.T, hankel[half:], precision=lax.Precision.HIGHEST, preferred_element_type=jnp.float32
    )
    share = order // (lax.axis_size("tm") * lax.axis_size("chan"))
    position = lax.axis_index(("tm", "chan"))
    mine = lax.dynamic_slice_in_dim(factor, position * share, share, 0)
    return (mine, states)


def solution(mesh):
    placed = (P("chan", "tm"), P())
    return jax.shard_map(
        per_device,
        mesh=mesh,
        in_specs=placed,
        out_specs=(P(("tm", "chan"), None), P(None, ("tm", "chan"))),
        check_vma=False,
    )
```

profile of v0, /device:TPU:1, one launch (start us, length us, event | category | flops | bytes accessed | tf_op | source)
XLA Modules:
  0.0 616.3 jit_solution(9280351724594159771)
XLA Ops:
  9.0 31.1 %all_to_all.19 = f32[16,4,8192]{2,0,1:T(8,128)S(1)} all-to-all(f32[16,4,8192]{2,0,1:T(8,128)S(1)} %bitcast.102), channel_id=1, replica_groups=mesh['tm'=32,'chan'=4] {'chan'}, dimensions={1} | all-to-all | bytes 4194304 | tf_op jit(solution)/shard_map/all_to_all | solution.py:31
  40.1 4.5 collective-permute-start
  80.8 5.7 copy-done.2
  86.5 118.2 %fusion.4 = f32[1024,1024]{0,1:T(8,128)} fusion(f32[1024,8192]{1,0:T(8,128)} %get-tuple-element.11, f32[8192]{0:T(1024)S(1)} %add_divide_fusion), kind=kOutput, calls=%fused_computation.21 | convolution fusion | flops 103088652288 | bytes 37781504 | tf_op jit(solution)/shard_map/dot_general | solution.py:21
  204.7 157.1 %all-reduce.3.cloned.1.call-done = f32[1024,1024]{0,1:T(8,128)} async-done(((f32[1024,1024]{0,1:T(8,128)}), f32[1024,1024]{0,1:T(8,128)}) %all-reduce.3.cloned.1.call-update) | async-done | bytes 4194320 | tf_op jit(solution)/shard_map/psum | solution.py:41
  361.8 5.3 copy.37
  367.2 4.4 fusion.3
  373.6 11.7 %cholesky.223 = f32[128,128]{1,0:T(8,128)S(1)} custom-call(f32[128,128]{1,0:T(8,128)S(1)} %cholesky.580), custom_call_target="Cholesky" | custom-call | tf_op jit(solution)/shard_map/jit(cholesky)/cholesky | solution.py:17
  385.4 9.8 %custom-call.59 = f32[1,128,128]{1,2,0:T(8,128)S(1)} custom-call(f32[1,128,128]{2,1,0:T(8,128)S(1)} %get-tuple-element.37), custom_call_target="InvertDiagBlocksLowerTriangular" | custom-call | tf_op jit(solution)/shard_map/jit(cholesky)/cholesky | solution.py:17
  401.4 12.1 %cholesky.244 = f32[128,128]{1,0:T(8,128)S(1)} custom-call(f32[128,128]{1,0:T(8,128)S(1)} %cholesky.584), custom_call_target="Cholesky" | custom-call | tf_op jit(solution)/shard_map/jit(cholesky)/cholesky | solution.py:17
  415.1 9.8 %custom-call.60 = f32[1,128,128]{1,2,0:T(8,128)S(1)} custom-call(f32[1,128,128]{2,1,0:T(8,128)S(1)} %get-tuple-element.34), custom_call_target="InvertDiagBlocksLowerTriangular" | custom-call | tf_op jit(solution)/shard_map/jit(cholesky)/cholesky | solution.py:17
  428.3 11.7 %cholesky.468 = f32[128,128]{1,0:T(8,128)S(1)} custom-call(f32[128,128]{1,0:T(8,128)S(1)} %cholesky.589), custom_call_target="Cholesky" | custom-call | tf_op jit(solution)/shard_map/jit(cholesky)/cholesky | solution.py:17
  441.3 9.8 %custom-call.61 = f32[1,128,128]{1,2,0:T(8,128)S(1)} custom-call(f32[1,128,128]{2,1,0:T(8,128)S(1)} %get-tuple-element.31), custom_call_target="InvertDiagBlocksLowerTriangular" | custom-call | tf_op jit(solution)/shard_map/jit(cholesky)/cholesky | solution.py:17
  454.6 11.9 %cholesky.487 = f32[128,128]{1,0:T(8,128)S(1)} custom-call(f32[128,128]{1,0:T(8,128)S(1)} %cholesky.594), custom_call_target="Cholesky" | custom-call | tf_op jit(solution)/shard_map/jit(cholesky)/cholesky | solution.py:17
  467.8 9.8 %custom-call.62 = f32[1,128,128]{1,2,0:T(8,128)S(1)} custom-call(f32[1,128,128]{2,1,0:T(8,128)S(1)} %get-tuple-element.28), custom_call_target="InvertDiagBlocksLowerTriangular" | custom-call | tf_op jit(solution)/shard_map/jit(cholesky)/cholesky | solution.py:17
  481.1 11.7 %cholesky.506 = f32[128,128]{1,0:T(8,128)S(1)} custom-call(f32[128,128]{1,0:T(8,128)S(1)} %cholesky.599), custom_call_target="Cholesky" | custom-call | tf_op jit(solution)/shard_map/jit(cholesky)/cholesky | solution.py:17
  494.1 10.0 %custom-call.63 = f32[1,128,128]{1,2,0:T(8,128)S(1)} custom-call(f32[1,128,128]{2,1,0:T(8,128)S(1)} %get-tuple-element.25), custom_call_target="InvertDiagBlocksLowerTriangular" | custom-call | tf_op jit(solution)/shard_map/jit(cholesky)/cholesky | solution.py:17
  507.4 11.7 %cholesky.526 = f32[128,128]{1,0:T(8,128)S(1)} custom-call(f32[128,128]{1,0:T(8,128)S(1)} %cholesky.604), custom_call_target="Cholesky" | custom-call | tf_op jit(solution)/shard_map/jit(cholesky)/cholesky | solution.py:17
  520.4 9.8 %custom-call.64 = f32[1,128,128]{1,2,0:T(8,128)S(1)} custom-call(f32[1,128,128]{2,1,0:T(8,128)S(1)} %get-tuple-element.22), custom_call_target="InvertDiagBlocksLowerTriangular" | custom-call | tf_op jit(solution)/shard_map/jit(cholesky)/cholesky | solution.py:17
  533.3 12.1 %cholesky.546 = f32[128,128]{1,0:T(8,128)S(1)} custom-call(f32[128,128]{1,0:T(8,128)S(1)} %cholesky.609), custom_call_target="Cholesky" | custom-call | tf_op jit(solution)/shard_map/jit(cholesky)/cholesky | solution.py:17
  546.6 9.8 %custom-call.65 = f32[1,128,128]{1,2,0:T(8,128)S(1)} custom-call(f32[1,128,128]{2,1,0:T(8,128)S(1)} %get-tuple-element.19), custom_call_target="InvertDiagBlocksLowerTriangular" | custom-call | tf_op jit(solution)/shard_map/jit(cholesky)/cholesky | solution.py:17
  559.1 11.7 %cholesky.564 = f32[128,128]{1,0:T(8,128)S(1)} custom-call(f32[128,128]{1,0:T(8,128)S(1)} %slice_subtract_fusion.6), custom_call_target="Cholesky" | custom-call | tf_op jit(solution)/shard_map/jit(cholesky)/cholesky | solution.py:17
  577.8 2.8 fusion.130
  594.0 15.2 %fusion.103 = f32[128,8192]{1,0:T(8,128)} fusion(f32[512,128]{1,0:T(8,128)S(1)} %fusion.31, f32[512,8192]{1,0:T(8,128)} %copy-done.2), kind=kOutput, calls=%fused_computation.168 | convolution fusion | flops 6442450944 | bytes 21233664 | tf_op jit(solution)/shard_map/dot_general | solution.py:57
  (90 shorter events, 88.2 us)
Async XLA Ops:
  7.2 576.6 %copy-start = (f32[512,128]{1,0:T(8,128)S(1)}, f32[512,128]{1,0:T(8,128)}, u32[]{:S(2)}) copy-start(f32[512,128]{1,0:T(8,128)} %param.3) | copy-start | bytes 786436
  7.2 354.6 %all-reduce.3.cloned.1.call-start = ((), (), s32[]{:S(2)}) async-start(), calls=%async_computation.1 | async-start | bytes 8388608 | tf_op jit(solution)/shard_map/psum | solution.py:41
  40.1 5.5 collective-permute-start
  80.8 5.7 copy-start.2
  371.6 2.0 copy-start.3
  577.8 3.5 copy-start.1
Sparse Core Ops, SparseCore 0:
  204.8 156.9 all-reduce.2
where the time goes:
time: 626 us; the launch traced here: 616 us
  other arithmetic  218 us (35%)
  matrix products  164 us (26%)
  waiting for transfers between devices  158 us (25%)
  blocking collectives  31.1 us (5%)
  local copies, waits for them, and re-layouts  21.1 us (3%)
  between operations  20.2 us (3%)
    another operation x30, other arithmetic, upper_factor(): return jnp.linalg.cholesky(gram).T  173 us
    psum x1, waiting for transfers between devices, per_device(): gram = lax.psum(gram, ('tm', 'chan'))  157 us
    dot_general x1, matrix products, outer_gram(): lax.dot_general(left, right, (((1,), (1,)), ((), ())), precision=lax.Prec...  118 us
    unnamed x20, other arithmetic  33 us
    all_to_all x1, blocking collectives, per_device(): lax.all_to_all(samples, 'chan', split_axis=1, concat_axis=0, tiled=True)  31.1 us
    another operation x14, matrix products, upper_factor(): return jnp.linalg.cholesky(gram).T  22.8 us
    dot_general x1, matrix products, per_device(): jnp.dot(basis.T, hankel[half:], precision=lax.Precision.HIGHEST, preferre...  15.2 us
  transfers between devices with their start and end apart: 2, of which 2 were waited for; matrix products, arithmetic and copies ran while one was open for 0% of the time, Pallas kernels for 0%

commit v1 on v0

v1 whole, which is shorter than its diff:
```python
import jax
import jax.numpy as jnp
from jax import lax
from jax.experimental import pallas as pl
from jax.experimental.pallas import tpu as pltpu
from jax.sharding import PartitionSpec as P

BR = 16
NSTEPS = 6
CH = 64
ORDER = 1024
HALF = 512
PANEL = 128
BLOCK = 256
PAD = 128
STEP = 512
TILES = 640
F32 = jnp.float32
BF16 = jnp.bfloat16
EXACT = lax.Precision.HIGHEST
ALL = ("tm", "chan")
NN = (((1,), (0,)), ((), ()))
NT = (((1,), (1,)), ((), ()))
TN = (((0,), (0,)), ((), ()))
VMEM = pl.BlockSpec(memory_space=pltpu.VMEM)
SMEM = pl.BlockSpec(memory_space=pltpu.SMEM)


def params():
    return pltpu.CompilerParams(vmem_limit_bytes=50 << 20)


def mul(left, right, dims, precision=None):
    return lax.dot_general(
        left, right, dims, precision=precision, preferred_element_type=F32
    )


def upper_tiles():
    for top in range(0, ORDER, BLOCK):
        for row in range(top, top + BLOCK, 8):
            for col in range(top, ORDER, 128):
                yield row, col


def split(value):
    high = value.astype(BF16)
    return high, (value - high.astype(F32)).astype(BF16)


def gram_kernel(place_ref, p0_ref, p1_ref, p2_ref, p3_ref, x_ref, packed_ref, h0, l0, h1, l1, g):
    count = x_ref.shape[1] - PAD
    group = CH // 4
    for away, piece in enumerate((p0_ref, p1_ref, p2_ref, p3_ref)):
        owner = (place_ref[0] + 4 - away) % 4
        x_ref[pl.ds(pl.multiple_of(owner * group, group), group), :] = piece[...]

    def prepare(start, high_ref, low_ref):
        window = x_ref[:, pl.ds(start, STEP + PAD)]
        first = window[:, :STEP]
        root = lax.rsqrt(1.0 + jnp.sum(first * first, 0, keepdims=True) * (1.0 / CH))
        for k in range(BR):
            high, low = split(window[:, k : k + STEP] * root)
            high_ref[k * CH : (k + 1) * CH, :] = high
            low_ref[k * CH : (k + 1) * CH, :] = low

    def accumulate(high_ref, low_ref):
        for top in range(0, ORDER, BLOCK):
            rows, cols = slice(top, top + BLOCK), slice(top, ORDER)
            term = mul(high_ref[rows, :], high_ref[cols, :], NT)
            term += mul(high_ref[rows, :], low_ref[cols, :], NT)
            term += mul(low_ref[rows, :], high_ref[cols, :], NT)
            g[rows, cols] += term

    g[...] = jnp.zeros_like(g)
    prepare(0, h0, l0)

    def pair(j, carry):
        base = j * (2 * STEP)
        prepare(pl.multiple_of(base + STEP, STEP), h1, l1)
        accumulate(h0, l0)
        after = jnp.minimum(base + 2 * STEP, count - STEP)
        prepare(pl.multiple_of(after, STEP), h0, l0)
        accumulate(h1, l1)
        return carry

    lax.fori_loop(0, count // (2 * STEP), pair, 0)
    scale = 1.0 / (count * 128)
    for index, (row, col) in enumerate(upper_tiles()):
        piece, at = divmod(index, TILES // 128)
        packed_ref[piece, 8 * at : 8 * at + 8, :] = g[row : row + 8, col : col + 128] * scale


def weighted_gram(place, pieces):
    group, width = pieces[0].shape
    count = width - PAD
    slab = pltpu.VMEM((ORDER, STEP), BF16)
    return pl.pallas_call(
        gram_kernel,
        out_shape=(
            jax.ShapeDtypeStruct((CH, width), F32),
            jax.ShapeDtypeStruct((128, 8 * TILES // 128, 128), F32),
        ),
        in_specs=[SMEM] + [VMEM] * 4,
        out_specs=(VMEM, VMEM),
        scratch_shapes=[slab] * 4 + [pltpu.VMEM((ORDER, ORDER), F32)],
        compiler_params=params(),
        name="gram",
    )(place, *pieces)


def lane(value, j):
    return jnp.broadcast_to(value[:, j : j + 1], (8, 128))


def row(value, j):
    return jnp.broadcast_to(value[j : j + 1, :], (8, 128))


def diagonal_factor(d):
    n = PANEL // 8
    rows = lax.broadcasted_iota(jnp.int32, (8, 128), 0)
    cols = lax.broadcasted_iota(jnp.int32, (8, 128), 1)
    w = [jnp.where(cols == rows + 8 * i, 1.0, 0.0).astype(F32) for i in range(n)]
    upper, inverse = [], []
    for g in range(n):
        cg = [lane(d[g], 8 * g + j) for j in range(8)]
        below = range(g + 1, n)
        cb = {i: [lane(d[i], 8 * g + j) for j in range(8)] for i in below}
        dg, wg = d[g], w[g]
        tops, inv = [], []
        pivots = jnp.zeros((8, 128), F32)
        for j in range(8):
            pivot = row(cg[j], j)
            r = 1.0 / pivot
            inv.append(r)
            pivots = jnp.where(rows == j, pivot, pivots)
            m = jnp.where(rows > j, cg[j] * r, 0.0)
            top = {k: row(cg[k], j) for k in range(j + 1, 8)}
            tops.append(top)
            for k in range(j + 1, 8):
                cg[k] = cg[k] - m * top[k]
            dg = dg - m * row(dg, j)
            wg = wg - m * row(wg, j)
        scale = lax.rsqrt(pivots)
        upper.append(jnp.where(cols >= rows + 8 * g, dg * scale, 0.0))
        inverse.append(wg * scale)
        ds = [row(dg, j) for j in range(8)]
        ws = [row(wg, j) for j in range(8)]
        for i in below:
            c, di, wi = cb[i], d[i], w[i]
            for j in range(8):
                m = c[j] * inv[j]
                for k in range(j + 1, 8):
                    c[k] = c[k] - m * tops[j][k]
                di = di - m * ds[j]
                wi = wi - m * ws[j]
            d[i], w[i] = di, wi
    return upper, inverse


def factor_kernel(place_ref, packed_ref, start_ref, mine_ref, basis_ref, a, u, inverse_ref):
    p = pl.program_id(0)

    @pl.when(p == 0)
    def _():
        u[...] = jnp.zeros_like(u)
        for index, (r, c) in enumerate(upper_tiles()):
            piece, at = divmod(index, TILES // 128)
            a[r : r + 8, c : c + 128] = packed_ref[piece, 8 * at : 8 * at + 8, :]

    o = pl.multiple_of(p * PANEL, PANEL)
    strips = [pl.ds(pl.multiple_of(o + 8 * i, 8), 8) for i in range(PANEL // 8)]
    upper, inverse = diagonal_factor([a[s, pl.ds(o, PANEL)] for s in strips])
    for i, s in enumerate(strips):
        u[s, pl.ds(o, PANEL)] = upper[i]
        inverse_ref[8 * i : 8 * i + 8, :] = inverse[i]
    for q in range(ORDER // PANEL - 1):

        @pl.when(p == q)
        def _():
            top, s = q * PANEL, (q + 1) * PANEL
            panel = mul(inverse_ref[...], a[top:s, s:], NN, EXACT)
            u[top:s, s:] = panel
            for b in range(s, ORDER, BLOCK):
                e = min(b + BLOCK, ORDER)
                a[b:e, b:] -= mul(panel[:, b - s : e - s], panel[:, b - s :], TN, EXACT)

    @pl.when(p == ORDER // PANEL - 1)
    def _():
        share = mine_ref.shape[0]
        mine_ref[...] = u[pl.ds(pl.multiple_of(place_ref[0] * share, share), share), :]
        lead = mul(start_ref[...], u[HALF:, HALF:], TN, EXACT)
        basis = lead / jnp.sqrt(jnp.sum(lead * lead))
        inner = mul(basis, basis, NT, EXACT)
        states = inner.shape[0]
        eye = jnp.where(
            lax.broadcasted_iota(jnp.int32, (states, states), 0)
            == lax.broadcasted_iota(jnp.int32, (states, states), 1),
            1.5,
            0.0,
        ).astype(F32)
        total = None
        for step in range(NSTEPS):
            m = eye - 0.5 * inner
            total = m if total is None else mul(total, m, NN, EXACT)
            if step < NSTEPS - 1:
                inner = mul(mul(inner, m, NN, EXACT), m, NN, EXACT)
        basis_ref[...] = mul(total, basis, NN, EXACT)


def factor_and_basis(place, packed, start, share):
    whole = lambda shape: pl.BlockSpec(shape, lambda i: (0,) * len(shape))
    states = start.shape[1]
    return pl.pallas_call(
        factor_kernel,
        grid=(ORDER // PANEL,),
        out_shape=(
            jax.ShapeDtypeStruct((share, ORDER), F32),
            jax.ShapeDtypeStruct((states, HALF), F32),
        ),
        in_specs=[SMEM, whole(packed.shape), whole(start.shape)],
        out_specs=(whole((share, ORDER)), whole((states, HALF))),
        scratch_shapes=[
            pltpu.VMEM((ORDER, ORDER), F32),
            pltpu.VMEM((ORDER, ORDER), F32),
            pltpu.VMEM((PANEL, PANEL), F32),
        ],
        compiler_params=params(),
        name="factor",
    )(place, packed, start)


def states_kernel(basis_ref, x_ref, out_ref, high_ref, low_ref):
    span = out_ref.shape[1]
    start = pl.multiple_of(pl.program_id(0) * span, span)
    window = x_ref[:, pl.ds(start, span + PAD)]
    first = BR // 2
    for k in range(first):
        high, low = split(window[:, first + k : first + k + span])
        high_ref[k * CH : (k + 1) * CH, :] = high
        low_ref[k * CH : (k + 1) * CH, :] = low
    bh, bl = split(basis_ref[...])
    out = mul(bh, high_ref[...], NN)
    out += mul(bl, high_ref[...], NN)
    out_ref[...] = out + mul(bh, low_ref[...], NN)


def project(basis, x):
    states = basis.shape[0]
    count = x.shape[1] - PAD
    span = 1024
    slab = pltpu.VMEM((HALF, span), BF16)
    return pl.pallas_call(
        states_kernel,
        grid=(count // span,),
        out_shape=jax.ShapeDtypeStruct((states, count), F32),
        in_specs=[
            pl.BlockSpec(basis.shape, lambda i: (0, 0)),
            pl.BlockSpec(x.shape, lambda i: (0, 0)),
        ],
        out_specs=pl.BlockSpec((states, span), lambda i: (0, i)),
        scratch_shapes=[slab, slab],
        compiler_params=params(),
        name="states",
    )(basis, x)


def per_device(samples, start_basis):
    tms, chans = lax.axis_size("tm"), lax.axis_size("chan")
    count = samples.shape[1] // chans
    chan = lax.axis_index("chan")
    halo = lax.ppermute(samples[:, :PAD], "tm", [(i, i - 1) for i in range(1, tms)])
    extended = jnp.concatenate([samples, halo], 1)
    pieces = []
    for away in range(chans):
        to = (chan + away) % chans
        window = lax.dynamic_slice_in_dim(extended, to * count, count + PAD, 1)
        if away:
            window = lax.ppermute(window, "chan", [(i, (i + away) % chans) for i in range(chans)])
        pieces.append(window)
    x, packed = weighted_gram(chan[None].astype(jnp.int32), pieces)
    packed = lax.all_to_all(packed, ALL, 0, 0, tiled=True)
    total = jnp.sum(packed, 0)
    packed = jnp.broadcast_to(total[None], packed.shape)
    packed = lax.all_to_all(packed, ALL, 0, 0, tiled=True)
    position = lax.axis_index(ALL)[None].astype(jnp.int32)
    mine, basis = factor_and_basis(position, packed, start_basis, ORDER // (tms * chans))
    return (mine, project(basis, x))


def solution(mesh):
    return jax.shard_map(
        per_device,
        mesh=mesh,
        in_specs=(P("chan", "tm"), P()),
        out_specs=(P(ALL, None), P(None, ALL)),
        check_vma=False,
    )
```

time: 626 us -> 219 us (0.35); the launches traced: 616 us -> 219 us
  other arithmetic: 218 us -> 0.21 us
  matrix products: 164 us -> 0 us
  waiting for transfers between devices: 158 us -> 62.6 us
  Pallas kernels: 0 us -> 94.5 us
  between operations: 20.2 us -> 0.73 us
  local copies, waits for them, and re-layouts: 21.1 us -> 4.24 us
  blocking collectives: 31.1 us -> 44.4 us
  starting transfers between devices: 4.57 us -> 11.8 us
    another operation x30 -> x0, other arithmetic: 173 us -> none  [upper_factor(): return jnp.linalg.cholesky(gram).T]
    psum x1 -> x0, waiting for transfers between devices: 157 us -> none  [per_device(): gram = lax.psum(gram, ('tm', 'chan'))]
    dot_general x15 -> x0, matrix products: 141 us -> none  [the longest x1 118 us: outer_gram(): lax.dot_general(left, right, (((1,), (1,)), ((), ())), precision=lax.Prec...]
    pallas_call x0 -> x3, Pallas kernels: none -> 94.5 us  [the longest x1 47.3 us: factor_and_basis(): pl.pallas_call(factor_kernel, grid=(ORDER // PANEL,), out_shape=(jax.Shap...]
    all_to_all x0 -> x1, waiting for transfers between devices: none -> 36.6 us  [per_device(): packed = lax.all_to_all(packed, ALL, 0, 0, tiled=True)]
    unnamed x20 -> x0, other arithmetic: 33 us -> none
    ppermute x1 -> x4, waiting for transfers between devices: 0.78 us -> 26 us  [the longest x3 25.2 us: per_device(): lax.ppermute(window, 'chan', [(i, (i + away) % chans) for i in range(chan...]
    another operation x14 -> x0, matrix products: 22.8 us -> none  [upper_factor(): return jnp.linalg.cholesky(gram).T]
  transfers between devices with their start and end apart: 2 -> 5, of which waited for: 2 -> 4; matrix products, arithmetic and copies ran while one was open for 0% -> 1% of each run, Pallas kernels for 0% -> 0%
where the time goes in v1:
time: 219 us
  Pallas kernels  94.5 us (43%)
  waiting for transfers between devices  62.6 us (29%)
  blocking collectives  44.4 us (20%)
  starting transfers between devices  11.8 us (5%)
  local copies, waits for them, and re-layouts  4.24 us (2%)
    pallas_call x1, Pallas kernels, factor_and_basis(): pl.pallas_call(factor_kernel, grid=(ORDER // PANEL,), out_shape=(jax.Shap...  47.3 us
    all_to_all x1, blocking collectives, per_device(): packed = lax.all_to_all(packed, ALL, 0, 0, tiled=True)  44.4 us
    pallas_call x1, Pallas kernels, weighted_gram(): pl.pallas_call(gram_kernel, out_shape=(jax.ShapeDtypeStruct((CH, width),...  38.4 us
    all_to_all x1, waiting for transfers between devices, per_device(): packed = lax.all_to_all(packed, ALL, 0, 0, tiled=True)  36.6 us
    ppermute x3, waiting for transfers between devices, per_device(): lax.ppermute(window, 'chan', [(i, (i + away) % chans) for i in range(chan...  25.2 us
    pallas_call x1, Pallas kernels, project(): pl.pallas_call(states_kernel, grid=(count // span,), out_shape=jax.ShapeD...  8.87 us
    ppermute x3, starting transfers between devices, per_device(): lax.ppermute(window, 'chan', [(i, (i + away) % chans) for i in range(chan...  4.53 us
  transfers between devices with their start and end apart: 5, of which 4 were waited for; matrix products, arithmetic and copies ran while one was open for 1% of the time, Pallas kernels for 0%

profile of v1, /device:TPU:1, one launch (start us, length us, event | category | flops | bytes accessed | tf_op | source)
XLA Modules:
  0.0 218.5 jit_solution(4870964942984598986)
XLA Ops:
  0.6 0.7 slice.3
  1.3 3.3 %collective-permute-start = (f32[16,128]{1,0:T(8,128)S(1)}, f32[16,128]{1,0:T(8,128)S(1)}, u32[]{:S(2)}, u32[]{:S(2)}) collective-permute-start(f32[16,128]{1,0:T(8,128)S(1)} %slice.3), channel_id=1, source_target_pairs={{4,0},{8,4},{12,8},{16,12},{20,16},{24,20},{28,24},{32,28},{36,32}... | collective-permute-start | bytes 24584 | tf_op jit(solution)/shard_map/ppermute | solution.py:273
  4.7 1.7 constant_dynamic-update-slice_fusion.1
  6.4 0.8 collective-permute-done
  7.2 0.1 constant_dynamic-slice_fusion
  7.4 3.8 %collective-permute-start.3 = (f32[16,8320]{1,0:T(8,128)S(1)}, f32[16,8320]{1,0:T(8,128)S(1)}, u32[]{:S(2)}, u32[]{:S(2)}) collective-permute-start(f32[16,8320]{1,0:T(8,128)S(1)} %get-tuple-element.10), channel_id=1, source_target_pairs={{0,3},{1,0},{2,1},{3,2},{4,7},{5,4},{6,5},{7,6},{8,11},{9,8},{10,9... | collective-permute-start | bytes 1597448 | tf_op jit(solution)/shard_map/ppermute | solution.py:280
  11.2 0.0 collective-permute-start.2
  11.2 0.7 collective-permute-start.1
  11.9 21.8 %collective-permute-done.3.p3_ref = f32[16,8320]{1,0:T(8,128)S(1)} collective-permute-done((f32[16,8320]{1,0:T(8,128)S(1)}, f32[16,8320]{1,0:T(8,128)S(1)}, u32[]{:S(2)}, u32[]{:S(2)}) %collective-permute-start.3) | collective-permute-done | bytes 532512 | tf_op jit(solution)/shard_map/ppermute | solution.py:280
  33.7 0.0 collective-permute-done.2.p2_ref
  33.7 3.4 %collective-permute-done.1.p1_ref = f32[16,8320]{1,0:T(8,128)S(1)} collective-permute-done((f32[16,8320]{1,0:T(8,128)S(1)}, f32[16,8320]{1,0:T(8,128)S(1)}, u32[]{:S(2)}, u32[]{:S(2)}) %collective-permute-start.1) | collective-permute-done | bytes 532512 | tf_op jit(solution)/shard_map/ppermute | solution.py:280
  37.1 38.4 %gram.1 = (f32[64,8320]{1,0:T(8,128)}, f32[128,40,128]{2,1,0:T(8,128)}) custom-call(s32[1]{0:T(128)} %bitcast.1.place_ref, f32[16,8320]{1,0:T(8,128)S(1)} %get-tuple-element.13.p0_ref, f32[16,8320]{1,0:T(8,128)S(1)} %collective-permute-done.1.p1_ref, f32[16,8320]{1,0:T(8,128)S(1)} %collective-permute-done.2.p2_ref, f32[16,8320]{1,0:T(8,128)S(1)} %collective-permute-done.3.p3_ref), custom_call_target="tpu_custom_call" | custom-call | tf_op jit(solution)/shard_map/gram/pallas_call | solution.py:98
  75.5 44.4 %all_to_all.10 = f32[128,40,128]{2,1,0:T(8,128)S(1)} all-to-all(f32[128,40,128]{2,1,0:T(8,128)} %get-tuple-element.6), channel_id=1, replica_groups=mesh['tm'=32,'chan'=4] {'tm','chan'}, dimensions={0} | all-to-all | bytes 5242880 | tf_op jit(solution)/shard_map/all_to_all | solution.py:283
  119.9 0.2 reduce_sum.9
  120.1 1.7 broadcast_in_dim.14
  121.8 0.0 copy-start.1
  121.8 4.0 %all-to-all-start.1 = ((f32[128,40,128]{2,1,0:T(8,128)}), f32[128,40,128]{2,1,0:T(8,128)S(1)}, u32[]{:S(2)}, u32[]{:S(2)}) async-start(f32[128,40,128]{2,1,0:T(8,128)} %broadcast_in_dim.14), calls=%async_computation.1 | async-start | bytes 5242880 | tf_op jit(solution)/shard_map/all_to_all | solution.py:286
  125.8 36.6 %all-to-all-done.1.packed_ref = f32[128,40,128]{2,1,0:T(8,128)S(1)} async-done(((f32[128,40,128]{2,1,0:T(8,128)}), f32[128,40,128]{2,1,0:T(8,128)S(1)}, u32[]{:S(2)}, u32[]{:S(2)}) %all-to-all-start.1) | async-done | bytes 2621472 | tf_op jit(solution)/shard_map/all_to_all | solution.py:286
  162.4 0.0 copy-start
  162.4 0.0 copy-done.1
  162.4 47.3 %factor.1 = (f32[8,1024]{1,0:T(8,128)}, f32[128,512]{1,0:T(8,128)S(1)}) custom-call(s32[1]{0:T(128)} %bitcast.place_ref, f32[128,40,128]{2,1,0:T(8,128)S(1)} %all-to-all-done.1.packed_ref, f32[512,128]{1,0:T(8,128)S(1)} %copy-done.1), custom_call_target="tpu_custom_call" | custom-call | tf_op jit(solution)/shard_map/factor/pallas_call | solution.py:215
  209.7 0.0 copy-done
  209.7 8.9 %states.1 = f32[128,8192]{1,0:T(8,128)} custom-call(f32[128,512]{1,0:T(8,128)S(1)} %get-tuple-element.8.basis_ref, f32[64,8320]{1,0:T(8,128)S(1)} %copy-done), custom_call_target="tpu_custom_call" | custom-call | tf_op jit(solution)/shard_map/states/pallas_call | solution.py:254
  (1 shorter events, 0.0 us)
Async XLA Ops:
  1.3 5.9 %collective-permute-start = (f32[16,128]{1,0:T(8,128)S(1)}, f32[16,128]{1,0:T(8,128)S(1)}, u32[]{:S(2)}, u32[]{:S(2)}) collective-permute-start(f32[16,128]{1,0:T(8,128)S(1)} %slice.3), channel_id=1, source_target_pairs={{4,0},{8,4},{12,8},{16,12},{20,16},{24,20},{28,24},{32,28},{36,32}... | collective-permute-start | bytes 24584 | tf_op jit(solution)/shard_map/ppermute | solution.py:273
  7.4 26.3 %collective-permute-start.3 = (f32[16,8320]{1,0:T(8,128)S(1)}, f32[16,8320]{1,0:T(8,128)S(1)}, u32[]{:S(2)}, u32[]{:S(2)}) collective-permute-start(f32[16,8320]{1,0:T(8,128)S(1)} %get-tuple-element.10), channel_id=1, source_target_pairs={{0,3},{1,0},{2,1},{3,2},{4,7},{5,4},{6,5},{7,6},{8,11},{9,8},{10,9... | collective-permute-start | bytes 1597448 | tf_op jit(solution)/shard_map/ppermute | solution.py:280
  11.2 22.5 %collective-permute-start.2 = (f32[16,8320]{1,0:T(8,128)S(1)}, f32[16,8320]{1,0:T(8,128)S(1)}, u32[]{:S(2)}, u32[]{:S(2)}) collective-permute-start(f32[16,8320]{1,0:T(8,128)S(1)} %get-tuple-element.11), channel_id=1, source_target_pairs={{0,2},{1,3},{2,0},{3,1},{4,6},{5,7},{6,4},{7,5},{8,10},{9,11},{10,... | collective-permute-start | bytes 1597448 | tf_op jit(solution)/shard_map/ppermute | solution.py:280
  11.2 25.9 %collective-permute-start.1 = (f32[16,8320]{1,0:T(8,128)S(1)}, f32[16,8320]{1,0:T(8,128)S(1)}, u32[]{:S(2)}, u32[]{:S(2)}) collective-permute-start(f32[16,8320]{1,0:T(8,128)S(1)} %get-tuple-element.12), channel_id=1, source_target_pairs={{0,1},{1,2},{2,3},{3,0},{4,5},{5,6},{6,7},{7,4},{8,9},{9,10},{10,1... | collective-permute-start | bytes 1597448 | tf_op jit(solution)/shard_map/ppermute | solution.py:280
  121.8 40.6 %copy-start.1 = (f32[512,128]{1,0:T(8,128)S(1)}, f32[512,128]{1,0:T(8,128)}, u32[]{:S(2)}) copy-start(f32[512,128]{1,0:T(8,128)} %start_ref.1) | copy-start | bytes 786436
  121.8 40.6 %all-to-all-start.1 = ((f32[128,40,128]{2,1,0:T(8,128)}), f32[128,40,128]{2,1,0:T(8,128)S(1)}, u32[]{:S(2)}, u32[]{:S(2)}) async-start(f32[128,40,128]{2,1,0:T(8,128)} %broadcast_in_dim.14), calls=%async_computation.1 | async-start | bytes 5242880 | tf_op jit(solution)/shard_map/all_to_all | solution.py:286
  162.4 47.3 %copy-start = (f32[64,8320]{1,0:T(8,128)S(1)}, f32[64,8320]{1,0:T(8,128)}, u32[]{:S(2)}) copy-start(f32[64,8320]{1,0:T(8,128)} %get-tuple-element.9.x_ref) | copy-start | bytes 6389764

commit v2 on v1

--- a/solution.py
+++ b/solution.py
@@ -1,8 +1,11 @@
+import functools
+
 import jax
 import jax.numpy as jnp
 from jax import lax
 from jax.experimental import pallas as pl
 from jax.experimental.pallas import tpu as pltpu
+from jax.sharding import Mesh
 from jax.sharding import PartitionSpec as P
 
 BR = 16
@@ -14,11 +17,14 @@
 BLOCK = 256
 PAD = 128
 STEP = 512
+CHUNK = 3072
 TILES = 640
 F32 = jnp.float32
 BF16 = jnp.bfloat16
 EXACT = lax.Precision.HIGHEST
-ALL = ("tm", "chan")
+ALL = ("x", "y", "core", "chan")
+TIME = ("x", "y", "core")
+CHIPS = ("x", "y", "chan")
 NN = (((1,), (0,)), ((), ()))
 NT = (((1,), (1,)), ((), ()))
 TN = (((0,), (0,)), ((), ()))
@@ -26,8 +32,8 @@
 SMEM = pl.BlockSpec(memory_space=pltpu.SMEM)
 
 
-def params():
-    return pltpu.CompilerParams(vmem_limit_bytes=50 << 20)
+def params(mebibytes):
+    return pltpu.CompilerParams(vmem_limit_bytes=mebibytes << 20)
 
 
 def mul(left, right, dims, precision=None):
@@ -48,15 +54,21 @@
     return high, (value - high.astype(F32)).astype(BF16)
 
 
-def gram_kernel(place_ref, p0_ref, p1_ref, p2_ref, p3_ref, x_ref, packed_ref, h0, l0, h1, l1, g):
-    count = x_ref.shape[1] - PAD
+def gram_kernel(size, start, place_ref, p0_ref, p1_ref, p2_ref, p3_ref, *refs):
+    if start is None:
+        x_ref, out_ref, h0, l0, h1, l1, g, cross = refs
+        base = 0
+    else:
+        before_ref, sofar_ref, x_ref, keep_ref, send_ref, h0, l0, h1, l1, g, cross = refs
+        base = start
+        x_ref[:, :start] = before_ref[:, :start]
     group = CH // 4
     for away, piece in enumerate((p0_ref, p1_ref, p2_ref, p3_ref)):
         owner = (place_ref[0] + 4 - away) % 4
-        x_ref[pl.ds(pl.multiple_of(owner * group, group), group), :] = piece[...]
-
-    def prepare(start, high_ref, low_ref):
-        window = x_ref[:, pl.ds(start, STEP + PAD)]
+        x_ref[pl.ds(pl.multiple_of(owner * group, group), group), base:] = piece[...]
+
+    def prepare(at, high_ref, low_ref):
+        window = x_ref[:, pl.ds(at, STEP + PAD)]
         first = window[:, :STEP]
         root = lax.rsqrt(1.0 + jnp.sum(first * first, 0, keepdims=True) * (1.0 / CH))
         for k in range(BR):
@@ -65,48 +77,74 @@
             low_ref[k * CH : (k + 1) * CH, :] = low
 
     def accumulate(high_ref, low_ref):
-        for top in range(0, ORDER, BLOCK):
-            rows, cols = slice(top, top + BLOCK), slice(top, ORDER)
-            term = mul(high_ref[rows, :], high_ref[cols, :], NT)
-            term += mul(high_ref[rows, :], low_ref[cols, :], NT)
-            term += mul(low_ref[rows, :], high_ref[cols, :], NT)
-            g[rows, cols] += term
-
-    g[...] = jnp.zeros_like(g)
-    prepare(0, h0, l0)
+        for index, top in enumerate(range(0, ORDER, BLOCK)):
+            end = top + BLOCK
+            rows, cols = slice(top, end), slice(top, ORDER)
+            both = mul(high_ref[rows, :], high_ref[cols, :], NT)
+            mixed = mul(high_ref[rows, :], low_ref[cols, :], NT)
+            g[rows, rows] += both[:, :BLOCK]
+            cross[index] += mixed[:, :BLOCK]
+            if end < ORDER:
+                rest = slice(end, ORDER)
+                other = mul(low_ref[rows, :], high_ref[rest, :], NT)
+                g[rows, rest] += both[:, BLOCK:] + mixed[:, BLOCK:] + other
+
+    g[...] = jnp.zeros_like(g) if start is None else sofar_ref[...]
+    cross[...] = jnp.zeros_like(cross)
+    prepare(base, h0, l0)
 
     def pair(j, carry):
-        base = j * (2 * STEP)
-        prepare(pl.multiple_of(base + STEP, STEP), h1, l1)
+        at = base + j * (2 * STEP)
+        prepare(pl.multiple_of(at + STEP, STEP), h1, l1)
         accumulate(h0, l0)
-        after = jnp.minimum(base + 2 * STEP, count - STEP)
+        after = jnp.minimum(at + 2 * STEP, base + size - STEP)
         prepare(pl.multiple_of(after, STEP), h0, l0)
         accumulate(h1, l1)
         return carry
 
-    lax.fori_loop(0, count // (2 * STEP), pair, 0)
-    scale = 1.0 / (count * 128)
-    for index, (row, col) in enumerate(upper_tiles()):
-        piece, at = divmod(index, TILES // 128)
-        packed_ref[piece, 8 * at : 8 * at + 8, :] = g[row : row + 8, col : col + 128] * scale
-
-
-def weighted_gram(place, pieces):
+    lax.fori_loop(0, size // (2 * STEP), pair, 0)
+    for index, top in enumerate(range(0, ORDER, BLOCK)):
+        rows = slice(top, top + BLOCK)
+        g[rows, rows] += cross[index] + cross[index].T
+    if start is None:
+        out_ref[...] = g[...]
+        return
+    scale = 1.0 / ((base + size) * 128)
+    for core in range(2):
+
+        @pl.when(place_ref[1] == core)
+        def _():
+            for tile, (row, col) in enumerate(upper_tiles()):
+                half, piece, at = where(tile)
+                to_ref = keep_ref if half == core else send_ref
+                to_ref[piece, at : at + 8, :] = g[row : row + 8, col : col + 128] * scale
+
+
+def where(tile):
+    piece, at = divmod(tile, TILES // 128)
+    return piece // 64, piece % 64, 8 * at
+
+
+def gram_chunk(place, pieces, before=None):
     group, width = pieces[0].shape
-    count = width - PAD
+    size = width - PAD
     slab = pltpu.VMEM((ORDER, STEP), BF16)
+    gram = jax.ShapeDtypeStruct((ORDER, ORDER), F32)
+    half = jax.ShapeDtypeStruct((64, 8 * TILES // 128, 128), F32)
+    start = None if before is None else before[0].shape[1] - PAD
+    given = [] if before is None else list(before)
+    x = jax.ShapeDtypeStruct((CH, width + (start or 0)), F32)
+    out = (x, gram) if start is None else (x, half, half)
     return pl.pallas_call(
-        gram_kernel,
-        out_shape=(
-            jax.ShapeDtypeStruct((CH, width), F32),
-            jax.ShapeDtypeStruct((128, 8 * TILES // 128, 128), F32),
-        ),
-        in_specs=[SMEM] + [VMEM] * 4,
-        out_specs=(VMEM, VMEM),
-        scratch_shapes=[slab] * 4 + [pltpu.VMEM((ORDER, ORDER), F32)],
-        compiler_params=params(),
-        name="gram",
-    )(place, *pieces)
+        functools.partial(gram_kernel, size, start),
+        out_shape=out,
+        in_specs=[SMEM] + [VMEM] * (4 + len(given)),
+        out_specs=(VMEM,) * len(out),
+        scratch_shapes=[slab] * 4
+        + [pltpu.VMEM((ORDER, ORDER), F32), pltpu.VMEM((ORDER // BLOCK, BLOCK, BLOCK), F32)],
+        compiler_params=params(32),
+        name="gram_first" if start is None else "gram_last",
+    )(place, *pieces, *given)
 
 
 def lane(value, j):
@@ -159,15 +197,20 @@
     return upper, inverse
 
 
-def factor_kernel(place_ref, packed_ref, start_ref, mine_ref, basis_ref, a, u, inverse_ref):
+def factor_kernel(place_ref, own_ref, other_ref, start_ref, mine_ref, basis_ref, a, u, inverse_ref):
     p = pl.program_id(0)
 
     @pl.when(p == 0)
     def _():
         u[...] = jnp.zeros_like(u)
-        for index, (r, c) in enumerate(upper_tiles()):
-            piece, at = divmod(index, TILES // 128)
-            a[r : r + 8, c : c + 128] = packed_ref[piece, 8 * at : 8 * at + 8, :]
+        for core in range(2):
+
+            @pl.when(place_ref[1] == core)
+            def _():
+                for tile, (r, c) in enumerate(upper_tiles()):
+                    half, piece, at = where(tile)
+                    from_ref = own_ref if half == core else other_ref
+                    a[r : r + 8, c : c + 128] = from_ref[piece, at : at + 8, :]
 
     o = pl.multiple_of(p * PANEL, PANEL)
     strips = [pl.ds(pl.multiple_of(o + 8 * i, 8), 8) for i in range(PANEL // 8)]
@@ -209,7 +252,7 @@
         basis_ref[...] = mul(total, basis, NN, EXACT)
 
 
-def factor_and_basis(place, packed, start, share):
+def factor_and_basis(place, own, other, start, share):
     whole = lambda shape: pl.BlockSpec(shape, lambda i: (0,) * len(shape))
     states = start.shape[1]
     return pl.pallas_call(
@@ -219,16 +262,16 @@
             jax.ShapeDtypeStruct((share, ORDER), F32),
             jax.ShapeDtypeStruct((states, HALF), F32),
         ),
-        in_specs=[SMEM, whole(packed.shape), whole(start.shape)],
+        in_specs=[SMEM, whole(own.shape), whole(other.shape), whole(start.shape)],
         out_specs=(whole((share, ORDER)), whole((states, HALF))),
         scratch_shapes=[
             pltpu.VMEM((ORDER, ORDER), F32),
             pltpu.VMEM((ORDER, ORDER), F32),
             pltpu.VMEM((PANEL, PANEL), F32),
         ],
-        compiler_params=params(),
+        compiler_params=params(32),
         name="factor",
-    )(place, packed, start)
+    )(place, own, other, start)
 
 
 def states_kernel(basis_ref, x_ref, out_ref, high_ref, low_ref):
@@ -261,39 +304,52 @@
         ],
         out_specs=pl.BlockSpec((states, span), lambda i: (0, i)),
         scratch_shapes=[slab, slab],
-        compiler_params=params(),
+        compiler_params=params(32),
         name="states",
     )(basis, x)
 
 
-def per_device(samples, start_basis):
-    tms, chans = lax.axis_size("tm"), lax.axis_size("chan")
-    count = samples.shape[1] // chans
+def from_chans(array, starts, width):
+    chans = lax.axis_size("chan")
     chan = lax.axis_index("chan")
-    halo = lax.ppermute(samples[:, :PAD], "tm", [(i, i - 1) for i in range(1, tms)])
-    extended = jnp.concatenate([samples, halo], 1)
     pieces = []
     for away in range(chans):
-        to = (chan + away) % chans
-        window = lax.dynamic_slice_in_dim(extended, to * count, count + PAD, 1)
+        window = lax.dynamic_slice_in_dim(array, starts((chan + away) % chans), width, 1)
         if away:
             window = lax.ppermute(window, "chan", [(i, (i + away) % chans) for i in range(chans)])
         pieces.append(window)
-    x, packed = weighted_gram(chan[None].astype(jnp.int32), pieces)
-    packed = lax.all_to_all(packed, ALL, 0, 0, tiled=True)
-    total = jnp.sum(packed, 0)
-    packed = jnp.broadcast_to(total[None], packed.shape)
-    packed = lax.all_to_all(packed, ALL, 0, 0, tiled=True)
-    position = lax.axis_index(ALL)[None].astype(jnp.int32)
-    mine, basis = factor_and_basis(position, packed, start_basis, ORDER // (tms * chans))
+    return pieces
+
+
+def per_device(samples, start_basis):
+    times, chans = lax.axis_size(TIME), lax.axis_size("chan")
+    count = samples.shape[1] // chans
+    core = lax.axis_index("core")
+    place = jnp.stack([lax.axis_index("chan"), core]).astype(jnp.int32)
+    halo = lax.ppermute(samples[:, :PAD], TIME, [(i, i - 1) for i in range(1, times)])
+    pieces = from_chans(samples, lambda to: to * count, CHUNK + PAD)
+    extended = jnp.concatenate([samples, halo], 1)
+    pieces, extended = lax.optimization_barrier((pieces, extended))
+    others = from_chans(extended, lambda to: to * count + CHUNK, count - CHUNK + PAD)
+    first, sofar = gram_chunk(place, pieces)
+    x, keep, send = gram_chunk(place, others, (first, sofar))
+    swap = [(0, 1), (1, 0)]
+    half = keep + lax.ppermute(send, "core", swap)
+    half = lax.all_to_all(half, CHIPS, 0, 0, tiled=True)
+    half = jnp.broadcast_to(jnp.sum(half, 0)[None], half.shape)
+    half = lax.all_to_all(half, CHIPS, 0, 0, tiled=True)
+    other = lax.ppermute(half, "core", swap)
+    place = jnp.stack([lax.axis_index(ALL), core]).astype(jnp.int32)
+    mine, basis = factor_and_basis(place, half, other, start_basis, ORDER // (times * chans))
     return (mine, project(basis, x))
 
 
 def solution(mesh):
+    mesh = Mesh(mesh.devices.reshape(4, 4, 2, 4), ALL)
     return jax.shard_map(
         per_device,
         mesh=mesh,
-        in_specs=(P("chan", "tm"), P()),
+        in_specs=(P("chan", TIME), P()),
         out_specs=(P(ALL, None), P(None, ALL)),
         check_vma=False,
     )

time: 219 us -> 191 us (0.87)
  waiting for transfers between devices: 62.6 us -> 16.9 us
  blocking collectives: 44.4 us -> 54.1 us
  local copies, waits for them, and re-layouts: 4.24 us -> 8.23 us
    all_to_all x1 -> x0, waiting for transfers between devices: 36.6 us -> none  [per_device(): packed = lax.all_to_all(packed, ALL, 0, 0, tiled=True)]
    all_to_all x1 -> x2, blocking collectives: 44.4 us -> 54.1 us  [per_device(): half = lax.all_to_all(half, CHIPS, 0, 0, tiled=True)]
    ppermute x4 -> x9, waiting for transfers between devices: 26 us -> 16.9 us  [the longest x6 11.5 us: from_chans(): lax.ppermute(window, 'chan', [(i, (i + away) % chans) for i in range(chan...]
    ppermute x4 -> x9, starting transfers between devices: 7.84 us -> 13.8 us  [the longest x6 6.15 us: from_chans(): lax.ppermute(window, 'chan', [(i, (i + away) % chans) for i in range(chan...]
    unnamed x5 -> x14, local copies, waits for them, and re-layouts: 1.74 us -> 6.06 us
    all_to_all x1 -> x0, starting transfers between devices: 3.98 us -> none  [per_device(): packed = lax.all_to_all(packed, ALL, 0, 0, tiled=True)]
    pallas_call x1 -> x2, Pallas kernels: 38.4 us -> 36.7 us  [gram_chunk(): pl.pallas_call(functools.partial(gram_kernel, size, start), out_shape=out...]
  transfers between devices with their start and end apart: 5 -> 9, of which waited for: 4 -> 5; matrix products, arithmetic and copies ran while one was open for 1% -> 2% of each run, Pallas kernels for 0% -> 8%
where the time goes in v2:
time: 191 us; the launch traced here: 190 us
  Pallas kernels  94.3 us (49%)
  blocking collectives  54.1 us (28%)
  waiting for transfers between devices  16.9 us (9%)
  starting transfers between devices  13.8 us (7%)
  local copies, waits for them, and re-layouts  8.23 us (4%)
  other arithmetic  2.16 us (1%)
    all_to_all x2, blocking collectives, per_device(): half = lax.all_to_all(half, CHIPS, 0, 0, tiled=True)  54.1 us
    pallas_call x1, Pallas kernels, factor_and_basis(): pl.pallas_call(factor_kernel, grid=(ORDER // PANEL,), out_shape=(jax.Shap...  48.7 us
    pallas_call x2, Pallas kernels, gram_chunk(): pl.pallas_call(functools.partial(gram_kernel, size, start), out_shape=out...  36.7 us
    ppermute x6, waiting for transfers between devices, from_chans(): lax.ppermute(window, 'chan', [(i, (i + away) % chans) for i in range(chan...  11.5 us
    pallas_call x1, Pallas kernels, project(): pl.pallas_call(states_kernel, grid=(count // span,), out_shape=jax.ShapeD...  8.91 us
    ppermute x6, starting transfers between devices, from_chans(): lax.ppermute(window, 'chan', [(i, (i + away) % chans) for i in range(chan...  6.15 us
    unnamed x14, local copies, waits for them, and re-layouts  6.06 us
  transfers between devices with their start and end apart: 9, of which 5 were waited for; matrix products, arithmetic and copies ran while one was open for 2% of the time, Pallas kernels for 8%

profile of v2, /device:TPU:1, one launch (start us, length us, event | category | flops | bytes accessed | tf_op | source)
XLA Modules:
  0.0 190.3 jit_solution(13492878038417235114)
XLA Ops:
  1.3 3.3 %collective-permute-start.3 = (f32[16,128]{1,0:T(8,128)S(1)}, f32[16,128]{1,0:T(8,128)S(1)}, u32[]{:S(2)}, u32[]{:S(2)}) collective-permute-start(f32[16,128]{1,0:T(8,128)S(1)} %slice.3), channel_id=1, source_target_pairs={{4,0},{8,4},{12,8},{16,12},{20,16},{24,20},{28,24},{32,28},{36,32}... | collective-permute-start | bytes 24584 | tf_op jit(solution)/shard_map/ppermute | solution.py:329
  4.7 1.3 constant_dynamic-slice_fusion.4
  6.0 3.9 %collective-permute-start.2 = (f32[16,3200]{1,0:T(8,128)S(1)}, f32[16,3200]{1,0:T(8,128)S(1)}, u32[]{:S(2)}, u32[]{:S(2)}) collective-permute-start(f32[16,3200]{1,0:T(8,128)S(1)} %get-tuple-element.30), channel_id=1, source_target_pairs={{0,3},{1,0},{2,1},{3,2},{4,7},{5,4},{6,5},{7,6},{8,11},{9,8},{10,9... | collective-permute-start | bytes 614408 | tf_op jit(solution)/shard_map/ppermute | solution.py:319
  10.6 1.7 pad_maximum_fusion
  12.4 6.8 %collective-permute-done.2.p3_ref = f32[16,3200]{1,0:T(8,128)S(1)} collective-permute-done((f32[16,3200]{1,0:T(8,128)S(1)}, f32[16,3200]{1,0:T(8,128)S(1)}, u32[]{:S(2)}, u32[]{:S(2)}) %collective-permute-start.2) | collective-permute-done | bytes 204832 | tf_op jit(solution)/shard_map/ppermute | solution.py:319
  19.1 3.4 %collective-permute-done.p1_ref = f32[16,3200]{1,0:T(8,128)S(1)} collective-permute-done((f32[16,3200]{1,0:T(8,128)S(1)}, f32[16,3200]{1,0:T(8,128)S(1)}, u32[]{:S(2)}, u32[]{:S(2)}) %collective-permute-start) | collective-permute-done | bytes 204832 | tf_op jit(solution)/shard_map/ppermute | solution.py:319
  23.3 0.8 collective-permute-start.4
  24.2 14.7 %gram_first.1 = (f32[64,3200]{1,0:T(8,128)S(1)}, f32[1024,1024]{1,0:T(8,128)S(1)}) custom-call(s32[2]{0:T(128)S(1)} %pad_add_fusion.1.place_ref, f32[16,3200]{1,0:T(8,128)S(1)} %get-tuple-element.15.p0_ref, f32[16,3200]{1,0:T(8,128)S(1)} %collective-permute-done.p1_ref, f32[16,3200]{1,0:T(8,128)S(1)} %collective-permute-done.1.p2_ref, ...), custom_call_target="tpu_custom_call" | custom-call | tf_op jit(solution)/shard_map/gram_first/pallas_call | solution.py:138
  39.7 0.7 copy-done.2
  40.4 1.4 collective-permute-done.4.p1_ref
  41.8 0.7 copy-done.4
  42.5 1.0 copy-done.1
  43.5 1.0 copy-done.3
  44.5 1.0 copy-done.5
  45.4 22.0 %gram_last.1 = (f32[64,8320]{1,0:T(8,128)S(1)}, f32[64,40,128]{2,1,0:T(8,128)S(1)}, f32[64,40,128]{2,1,0:T(8,128)S(1)}) custom-call(s32[2]{0:T(128)S(1)} %pad_add_fusion.1.place_ref, f32[16,5248]{1,0:T(8,128)S(1)} %get-tuple-element.29.p0_ref, f32[16,5248]{1,0:T(8,128)S(1)} %copy-done.5, f32[16,5248]{1,0:T(8,128)S(1)} %copy-done.3, ...), custom_call_target="tpu_custom_call" | custom-call | tf_op jit(solution)/shard_map/gram_last/pallas_call | solution.py:138
  67.4 0.8 collective-permute-start.7
  68.2 2.7 %collective-permute-done.7 = f32[64,40,128]{2,1,0:T(8,128)S(1)} collective-permute-done((f32[64,40,128]{2,1,0:T(8,128)S(1)}, f32[64,40,128]{2,1,0:T(8,128)S(1)}, u32[]{:S(2)}, u32[]{:S(2)}) %collective-permute-start.7) | collective-permute-done | bytes 1310752 | tf_op jit(solution)/shard_map/ppermute | solution.py:337
  71.0 29.9 %all_to_all.10 = f32[64,40,128]{2,1,0:T(8,128)S(1)} all-to-all(f32[64,40,128]{2,1,0:T(8,128)S(1)} %add.107), channel_id=1, replica_groups=mesh['x'=4,'y'=4,'core'=2,'chan'=4] {'x','y','chan'}, dimensions={0} | all-to-all | bytes 2621440 | tf_op jit(solution)/shard_map/all_to_all | solution.py:338
  101.1 24.2 %all_to_all.11.own_ref = f32[64,40,128]{2,1,0:T(8,128)S(1)} all-to-all(f32[64,40,128]{2,1,0:T(8,128)S(1)} %broadcast_in_dim.2), channel_id=1, replica_groups=mesh['x'=4,'y'=4,'core'=2,'chan'=4] {'x','y','chan'}, dimensions={0} | all-to-all | bytes 2621440 | tf_op jit(solution)/shard_map/all_to_all | solution.py:340
  125.4 3.6 %collective-permute-start.8 = (f32[64,40,128]{2,1,0:T(8,128)S(1)}, f32[64,40,128]{2,1,0:T(8,128)}, u32[]{:S(2)}, u32[]{:S(2)}) collective-permute-start(f32[64,40,128]{2,1,0:T(8,128)S(1)} %all_to_all.11.own_ref), channel_id=1, source_target_pairs={{0,4},{4,0},{1,5},{5,1},{2,6},{6,2},{3,7},{7,3},{8,12},{12,8},{9,1... | collective-permute-start | bytes 3932168 | tf_op jit(solution)/shard_map/ppermute | solution.py:341
  129.0 2.7 %collective-permute-done.8.other_ref = f32[64,40,128]{2,1,0:T(8,128)} collective-permute-done((f32[64,40,128]{2,1,0:T(8,128)S(1)}, f32[64,40,128]{2,1,0:T(8,128)}, u32[]{:S(2)}, u32[]{:S(2)}) %collective-permute-start.8) | collective-permute-done | bytes 1310752 | tf_op jit(solution)/shard_map/ppermute | solution.py:341
  131.7 0.9 copy-done.6
  132.7 48.7 %factor.1 = (f32[8,1024]{1,0:T(8,128)}, f32[128,512]{1,0:T(8,128)S(1)}) custom-call(s32[2]{0:T(128)S(1)} %pad_add_fusion.place_ref, f32[64,40,128]{2,1,0:T(8,128)S(1)} %all_to_all.11.own_ref, f32[64,40,128]{2,1,0:T(8,128)} %collective-permute-done.8.other_ref, f32[512,128]{1,0:T(8,128)S(1)} %copy-done.6), custom_call_target="tpu_custom_call" | custom-call | tf_op jit(solution)/shard_map/factor/pallas_call | solution.py:258
  181.4 8.9 %states.1 = f32[128,8192]{1,0:T(8,128)} custom-call(f32[128,512]{1,0:T(8,128)S(1)} %get-tuple-element.24.basis_ref, f32[64,8320]{1,0:T(8,128)S(1)} %get-tuple-element.25.x_ref), custom_call_target="tpu_custom_call" | custom-call | tf_op jit(solution)/shard_map/states/pallas_call | solution.py:297
  (23 shorter events, 3.4 us)
Async XLA Ops:
  1.3 9.3 %collective-permute-start.3 = (f32[16,128]{1,0:T(8,128)S(1)}, f32[16,128]{1,0:T(8,128)S(1)}, u32[]{:S(2)}, u32[]{:S(2)}) collective-permute-start(f32[16,128]{1,0:T(8,128)S(1)} %slice.3), channel_id=1, source_target_pairs={{4,0},{8,4},{12,8},{16,12},{20,16},{24,20},{28,24},{32,28},{36,32}... | collective-permute-start | bytes 24584 | tf_op jit(solution)/shard_map/ppermute | solution.py:329
  6.0 13.1 %collective-permute-start.2 = (f32[16,3200]{1,0:T(8,128)S(1)}, f32[16,3200]{1,0:T(8,128)S(1)}, u32[]{:S(2)}, u32[]{:S(2)}) collective-permute-start(f32[16,3200]{1,0:T(8,128)S(1)} %get-tuple-element.30), channel_id=1, source_target_pairs={{0,3},{1,0},{2,1},{3,2},{4,7},{5,4},{6,5},{7,6},{8,11},{9,8},{10,9... | collective-permute-start | bytes 614408 | tf_op jit(solution)/shard_map/ppermute | solution.py:319
  9.9 9.2 %collective-permute-start.1 = (f32[16,3200]{1,0:T(8,128)S(1)}, f32[16,3200]{1,0:T(8,128)S(1)}, u32[]{:S(2)}, u32[]{:S(2)}) collective-permute-start(f32[16,3200]{1,0:T(8,128)S(1)} %get-tuple-element.31), channel_id=1, source_target_pairs={{0,2},{1,3},{2,0},{3,1},{4,6},{5,7},{6,4},{7,5},{8,10},{9,11},{10,... | collective-permute-start | bytes 614408 | tf_op jit(solution)/shard_map/ppermute | solution.py:319
  9.9 12.6 %collective-permute-start = (f32[16,3200]{1,0:T(8,128)S(1)}, f32[16,3200]{1,0:T(8,128)S(1)}, u32[]{:S(2)}, u32[]{:S(2)}) collective-permute-start(f32[16,3200]{1,0:T(8,128)S(1)} %get-tuple-element.32), channel_id=1, source_target_pairs={{0,1},{1,2},{2,3},{3,0},{4,5},{5,6},{6,7},{7,4},{8,9},{9,10},{10,1... | collective-permute-start | bytes 614408 | tf_op jit(solution)/shard_map/ppermute | solution.py:319
  22.6 16.3 %collective-permute-start.6 = (f32[16,5248]{1,0:T(8,128)S(1)}, f32[16,5248]{1,0:T(8,128)S(1)}, u32[]{:S(2)}, u32[]{:S(2)}) collective-permute-start(f32[16,5248]{1,0:T(8,128)S(1)} %get-tuple-element.26), channel_id=1, source_target_pairs={{0,3},{1,0},{2,1},{3,2},{4,7},{5,4},{6,5},{7,6},{8,11},{9,8},{10,9... | collective-permute-start | bytes 1007624 | tf_op jit(solution)/shard_map/ppermute | solution.py:319
  23.3 16.4 %collective-permute-start.5 = (f32[16,5248]{1,0:T(8,128)S(1)}, f32[16,5248]{1,0:T(8,128)S(1)}, u32[]{:S(2)}, u32[]{:S(2)}) collective-permute-start(f32[16,5248]{1,0:T(8,128)S(1)} %get-tuple-element.27), channel_id=1, source_target_pairs={{0,2},{1,3},{2,0},{3,1},{4,6},{5,7},{6,4},{7,5},{8,10},{9,11},{10,... | collective-permute-start | bytes 1007624 | tf_op jit(solution)/shard_map/ppermute | solution.py:319
  23.3 18.5 %collective-permute-start.4 = (f32[16,5248]{1,0:T(8,128)S(1)}, f32[16,5248]{1,0:T(8,128)S(1)}, u32[]{:S(2)}, u32[]{:S(2)}) collective-permute-start(f32[16,5248]{1,0:T(8,128)S(1)} %get-tuple-element.28), channel_id=1, source_target_pairs={{0,1},{1,2},{2,3},{3,0},{4,5},{5,6},{6,7},{7,4},{8,9},{9,10},{10,1... | collective-permute-start | bytes 1007624 | tf_op jit(solution)/shard_map/ppermute | solution.py:319
  38.9 0.7 copy-start
  39.7 0.7 copy-start.2
  41.8 0.7 copy-start.4
  42.5 1.0 copy-start.1
  43.5 1.0 copy-start.3
  44.5 1.0 copy-start.5
  67.4 3.4 %collective-permute-start.7 = (f32[64,40,128]{2,1,0:T(8,128)S(1)}, f32[64,40,128]{2,1,0:T(8,128)S(1)}, u32[]{:S(2)}, u32[]{:S(2)}) collective-permute-start(f32[64,40,128]{2,1,0:T(8,128)S(1)} %get-tuple-element.22), channel_id=1, source_target_pairs={{0,4},{4,0},{1,5},{5,1},{2,6},{6,2},{3,7},{7,3},{8,12},{12,8},{9,1... | collective-permute-start | bytes 3932168 | tf_op jit(solution)/shard_map/ppermute | solution.py:337
  125.4 6.3 %collective-permute-start.8 = (f32[64,40,128]{2,1,0:T(8,128)S(1)}, f32[64,40,128]{2,1,0:T(8,128)}, u32[]{:S(2)}, u32[]{:S(2)}) collective-permute-start(f32[64,40,128]{2,1,0:T(8,128)S(1)} %all_to_all.11.own_ref), channel_id=1, source_target_pairs={{0,4},{4,0},{1,5},{5,1},{2,6},{6,2},{3,7},{7,3},{8,12},{12,8},{9,1... | collective-permute-start | bytes 3932168 | tf_op jit(solution)/shard_map/ppermute | solution.py:341
  131.7 0.9 copy-start.6

commit v3 on v2

--- a/solution.py
+++ b/solution.py
@@ -30,6 +30,7 @@
 TN = (((0,), (0,)), ((), ()))
 VMEM = pl.BlockSpec(memory_space=pltpu.VMEM)
 SMEM = pl.BlockSpec(memory_space=pltpu.SMEM)
+HBM = pl.BlockSpec(memory_space=pltpu.HBM)
 
 
 def params(mebibytes):
@@ -56,16 +57,21 @@
 
 def gram_kernel(size, start, place_ref, p0_ref, p1_ref, p2_ref, p3_ref, *refs):
     if start is None:
-        x_ref, out_ref, h0, l0, h1, l1, g, cross = refs
+        x_ref, g, h0, l0, h1, l1, cross, sems = refs
         base = 0
+        first = pl.multiple_of(place_ref[0] * (p0_ref.shape[1] // 4), 128)
+        p0_ref = p0_ref.at[:, pl.ds(first, size + PAD)]
     else:
-        before_ref, sofar_ref, x_ref, keep_ref, send_ref, h0, l0, h1, l1, g, cross = refs
+        before_ref, sofar_ref, x_ref, keep_ref, send_ref, h0, l0, h1, l1, g, cross, sems = refs
         base = start
-        x_ref[:, :start] = before_ref[:, :start]
     group = CH // 4
+    copies = []
     for away, piece in enumerate((p0_ref, p1_ref, p2_ref, p3_ref)):
         owner = (place_ref[0] + 4 - away) % 4
-        x_ref[pl.ds(pl.multiple_of(owner * group, group), group), base:] = piece[...]
+        to = x_ref.at[pl.ds(pl.multiple_of(owner * group, group), group), pl.ds(base, size + PAD)]
+        copies.append(pltpu.make_async_copy(piece, to, sems.at[away]))
+    for copy in copies:
+        copy.start()
 
     def prepare(at, high_ref, low_ref):
         window = x_ref[:, pl.ds(at, STEP + PAD)]
@@ -89,8 +95,14 @@
                 other = mul(low_ref[rows, :], high_ref[rest, :], NT)
                 g[rows, rest] += both[:, BLOCK:] + mixed[:, BLOCK:] + other
 
-    g[...] = jnp.zeros_like(g) if start is None else sofar_ref[...]
     cross[...] = jnp.zeros_like(cross)
+    if start is None:
+        g[...] = jnp.zeros_like(g)
+    else:
+        g[...] = sofar_ref[...]
+        x_ref[:, :start] = before_ref[:, :start]
+    for copy in copies:
+        copy.wait()
     prepare(base, h0, l0)
 
     def pair(j, carry):
@@ -107,7 +119,6 @@
         rows = slice(top, top + BLOCK)
         g[rows, rows] += cross[index] + cross[index].T
     if start is None:
-        out_ref[...] = g[...]
         return
     scale = 1.0 / ((base + size) * 128)
     for core in range(2):
@@ -126,22 +137,23 @@
 
 
 def gram_chunk(place, pieces, before=None):
-    group, width = pieces[0].shape
-    size = width - PAD
+    size = pieces[1].shape[1] - PAD
     slab = pltpu.VMEM((ORDER, STEP), BF16)
     gram = jax.ShapeDtypeStruct((ORDER, ORDER), F32)
     half = jax.ShapeDtypeStruct((64, 8 * TILES // 128, 128), F32)
     start = None if before is None else before[0].shape[1] - PAD
     given = [] if before is None else list(before)
-    x = jax.ShapeDtypeStruct((CH, width + (start or 0)), F32)
+    pieces = [pltpu.with_memory_space_constraint(piece, pltpu.HBM) for piece in pieces]
+    x = jax.ShapeDtypeStruct((CH, size + PAD + (start or 0)), F32)
     out = (x, gram) if start is None else (x, half, half)
     return pl.pallas_call(
         functools.partial(gram_kernel, size, start),
         out_shape=out,
-        in_specs=[SMEM] + [VMEM] * (4 + len(given)),
+        in_specs=[SMEM] + [HBM] * 4 + [VMEM] * len(given),
         out_specs=(VMEM,) * len(out),
         scratch_shapes=[slab] * 4
-        + [pltpu.VMEM((ORDER, ORDER), F32), pltpu.VMEM((ORDER // BLOCK, BLOCK, BLOCK), F32)],
+        + ([] if start is None else [pltpu.VMEM((ORDER, ORDER), F32)])
+        + [pltpu.VMEM((ORDER // BLOCK, BLOCK, BLOCK), F32), pltpu.SemaphoreType.DMA((4,))],
         compiler_params=params(32),
         name="gram_first" if start is None else "gram_last",
     )(place, *pieces, *given)
@@ -197,12 +209,16 @@
     return upper, inverse
 
 
-def factor_kernel(place_ref, own_ref, other_ref, start_ref, mine_ref, basis_ref, a, u, inverse_ref):
+def factor_kernel(
+    place_ref, own_ref, other_ref, given_ref, mine_ref, basis_ref, a, u, inverse_ref, start_ref, sem
+):
     p = pl.program_id(0)
+    last = ORDER // PANEL - 1
+    fetch = pltpu.make_async_copy(given_ref, start_ref, sem.at[0])
 
     @pl.when(p == 0)
     def _():
-        u[...] = jnp.zeros_like(u)
+        fetch.start()
         for core in range(2):
 
             @pl.when(place_ref[1] == core)
@@ -225,14 +241,24 @@
             top, s = q * PANEL, (q + 1) * PANEL
             panel = mul(inverse_ref[...], a[top:s, s:], NN, EXACT)
             u[top:s, s:] = panel
+            high, low = split(panel)
             for b in range(s, ORDER, BLOCK):
-                e = min(b + BLOCK, ORDER)
-                a[b:e, b:] -= mul(panel[:, b - s : e - s], panel[:, b - s :], TN, EXACT)
-
-    @pl.when(p == ORDER // PANEL - 1)
+                rows, cols = slice(b - s, min(b + BLOCK, ORDER) - s), slice(b - s, ORDER - s)
+                term = mul(high[:, rows], high[:, cols], TN)
+                term += mul(high[:, rows], low[:, cols], TN)
+                a[b : b + BLOCK, b:] -= term + mul(low[:, rows], high[:, cols], TN)
+
+    @pl.when(p == last)
     def _():
         share = mine_ref.shape[0]
-        mine_ref[...] = u[pl.ds(pl.multiple_of(place_ref[0] * share, share), share), :]
+        top = pl.multiple_of(place_ref[0] * share, share)
+        below = lax.broadcasted_iota(jnp.int32, mine_ref.shape, 0) + top
+        cols = lax.broadcasted_iota(jnp.int32, mine_ref.shape, 1)
+        mine_ref[...] = jnp.where(cols >= below, u[pl.ds(top, share), :], 0.0)
+        for q in range(HALF // PANEL, last):
+            s = (q + 1) * PANEL
+            u[s:, q * PANEL : s] = jnp.zeros((ORDER - s, PANEL), F32)
+        fetch.wait()
         lead = mul(start_ref[...], u[HALF:, HALF:], TN, EXACT)
         basis = lead / jnp.sqrt(jnp.sum(lead * lead))
         inner = mul(basis, basis, NT, EXACT)
@@ -262,16 +288,18 @@
             jax.ShapeDtypeStruct((share, ORDER), F32),
             jax.ShapeDtypeStruct((states, HALF), F32),
         ),
-        in_specs=[SMEM, whole(own.shape), whole(other.shape), whole(start.shape)],
+        in_specs=[SMEM, whole(own.shape), whole(other.shape), HBM],
         out_specs=(whole((share, ORDER)), whole((states, HALF))),
         scratch_shapes=[
             pltpu.VMEM((ORDER, ORDER), F32),
             pltpu.VMEM((ORDER, ORDER), F32),
             pltpu.VMEM((PANEL, PANEL), F32),
+            pltpu.VMEM(start.shape, F32),
+            pltpu.SemaphoreType.DMA((1,)),
         ],
         compiler_params=params(32),
         name="factor",
-    )(place, own, other, start)
+    )(place, own, other, pltpu.with_memory_space_constraint(start, pltpu.HBM))
 
 
 def states_kernel(basis_ref, x_ref, out_ref, high_ref, low_ref):
@@ -292,7 +320,7 @@
 def project(basis, x):
     states = basis.shape[0]
     count = x.shape[1] - PAD
-    span = 1024
+    span = 2048
     slab = pltpu.VMEM((HALF, span), BF16)
     return pl.pallas_call(
         states_kernel,
@@ -309,16 +337,20 @@
     )(basis, x)
 
 
-def from_chans(array, starts, width):
+def windows(array, starts, width, nearest):
+    chans, chan = lax.axis_size("chan"), lax.axis_index("chan")
+    return [
+        lax.dynamic_slice_in_dim(array, starts((chan + away) % chans), width, 1)
+        for away in range(nearest, chans)
+    ]
+
+
+def exchange(owed):
     chans = lax.axis_size("chan")
-    chan = lax.axis_index("chan")
-    pieces = []
-    for away in range(chans):
-        window = lax.dynamic_slice_in_dim(array, starts((chan + away) % chans), width, 1)
-        if away:
-            window = lax.ppermute(window, "chan", [(i, (i + away) % chans) for i in range(chans)])
-        pieces.append(window)
-    return pieces
+    return [
+        lax.ppermute(window, "chan", [(i, (i + away) % chans) for i in range(chans)])
+        for away, window in enumerate(owed, 1)
+    ]
 
 
 def per_device(samples, start_basis):
@@ -326,12 +358,15 @@
     count = samples.shape[1] // chans
     core = lax.axis_index("core")
     place = jnp.stack([lax.axis_index("chan"), core]).astype(jnp.int32)
-    halo = lax.ppermute(samples[:, :PAD], TIME, [(i, i - 1) for i in range(1, times)])
-    pieces = from_chans(samples, lambda to: to * count, CHUNK + PAD)
+    owed = windows(samples, lambda to: to * count, CHUNK + PAD, 1)
+    owed, head = lax.optimization_barrier((owed, samples[:, :PAD]))
+    arrived = exchange(owed)
+    halo = lax.ppermute(head, TIME, [(i, i - 1) for i in range(1, times)])
     extended = jnp.concatenate([samples, halo], 1)
-    pieces, extended = lax.optimization_barrier((pieces, extended))
-    others = from_chans(extended, lambda to: to * count + CHUNK, count - CHUNK + PAD)
-    first, sofar = gram_chunk(place, pieces)
+    arrived, extended = lax.optimization_barrier((arrived, extended))
+    own, *owed = windows(extended, lambda to: to * count + CHUNK, count - CHUNK + PAD, 0)
+    others = [own] + exchange(owed)
+    first, sofar = gram_chunk(place, [samples] + arrived)
     x, keep, send = gram_chunk(place, others, (first, sofar))
     swap = [(0, 1), (1, 0)]
     half = keep + lax.ppermute(send, "core", swap)

time: 191 us -> 183 us (0.958)
  local copies, waits for them, and re-layouts: 8.23 us -> 3.54 us
  starting transfers between devices: 13.8 us -> 16.5 us
  waiting for transfers between devices: 16.9 us -> 14.2 us
    unnamed x14 -> x12, local copies, waits for them, and re-layouts: 6.06 us -> 0.73 us
    ppermute x7, waiting for transfers between devices: 11.5 us -> 8.79 us  [the longest x6 8.79 us: exchange(): lax.ppermute(window, 'chan', [(i, (i + away) % chans) for i in range(chan...]
    ppermute x7, starting transfers between devices: 9.47 us -> 12.1 us  [the longest x6 8.78 us: exchange(): lax.ppermute(window, 'chan', [(i, (i + away) % chans) for i in range(chan...]
    pallas_call x1, Pallas kernels: 48.7 us -> 46.1 us  [factor_and_basis(): pl.pallas_call(factor_kernel, grid=(ORDER // PANEL,), out_shape=(jax.Shap...]
    pallas_call x2, Pallas kernels: 36.7 us -> 38.9 us  [gram_chunk(): pl.pallas_call(functools.partial(gram_kernel, size, start), out_shape=out...]
  transfers between devices with their start and end apart: 9 -> 9, of which waited for: 5 -> 5; matrix products, arithmetic and copies ran while one was open for 2% -> 1% of each run, Pallas kernels for 8% -> 9%
where the time goes in v3:
time: 183 us
  Pallas kernels  92.6 us (51%)
  blocking collectives  53.2 us (29%)
  starting transfers between devices  16.5 us (9%)
  waiting for transfers between devices  14.2 us (8%)
  local copies, waits for them, and re-layouts  3.54 us (2%)
  other arithmetic  2.16 us (1%)
    all_to_all x2, blocking collectives, per_device(): half = lax.all_to_all(half, CHIPS, 0, 0, tiled=True)  53.2 us
    pallas_call x1, Pallas kernels, factor_and_basis(): pl.pallas_call(factor_kernel, grid=(ORDER // PANEL,), out_shape=(jax.Shap...  46.1 us
    pallas_call x2, Pallas kernels, gram_chunk(): pl.pallas_call(functools.partial(gram_kernel, size, start), out_shape=out...  38.9 us
    ppermute x6, waiting for transfers between devices, exchange(): lax.ppermute(window, 'chan', [(i, (i + away) % chans) for i in range(chan...  8.79 us
    ppermute x6, starting transfers between devices, exchange(): lax.ppermute(window, 'chan', [(i, (i + away) % chans) for i in range(chan...  8.78 us
    pallas_call x1, Pallas kernels, project(): pl.pallas_call(states_kernel, grid=(count // span,), out_shape=jax.ShapeD...  7.62 us
  transfers between devices with their start and end apart: 9, of which 5 were waited for; matrix products, arithmetic and copies ran while one was open for 1% of the time, Pallas kernels for 9%

profile of v3, /device:TPU:1, one launch (start us, length us, event | category | flops | bytes accessed | tf_op | source)
XLA Modules:
  0.0 182.9 jit_solution(11348653410916229331)
XLA Ops:
  0.7 0.7 slice.3
  1.4 1.2 constant_dynamic-slice_fusion.4
  2.5 3.3 %collective-permute-start.3 = (f32[16,128]{1,0:T(8,128)S(1)}, f32[16,128]{1,0:T(8,128)S(1)}, u32[]{:S(2)}, u32[]{:S(2)}) collective-permute-start(f32[16,128]{1,0:T(8,128)S(1)} %slice.3), channel_id=1, source_target_pairs={{4,0},{8,4},{12,8},{16,12},{20,16},{24,20},{28,24},{32,28},{36,32}... | collective-permute-start | bytes 24584 | tf_op jit(solution)/shard_map/ppermute | solution.py:364
  5.9 1.8 collective-permute-start
  7.7 3.3 %collective-permute-start.1 = (f32[16,3200]{1,0:T(8,128)S(1)}, f32[16,3200]{1,0:T(8,128)S(1)}, u32[]{:S(2)}, u32[]{:S(2)}) collective-permute-start(f32[16,3200]{1,0:T(8,128)S(1)} %get-tuple-element.18), channel_id=1, source_target_pairs={{0,2},{1,3},{2,0},{3,1},{4,6},{5,7},{6,4},{7,5},{8,10},{9,11},{10,... | collective-permute-start | bytes 614408 | tf_op jit(solution)/shard_map/ppermute | solution.py:351
  11.0 0.7 collective-permute-start.2
  11.7 1.7 pad_maximum_fusion
  13.4 1.3 collective-permute-done.p1_ref
  14.7 6.0 %collective-permute-done.1.p2_ref = f32[16,3200]{1,0:T(8,128)S(1)} collective-permute-done((f32[16,3200]{1,0:T(8,128)S(1)}, f32[16,3200]{1,0:T(8,128)S(1)}, u32[]{:S(2)}, u32[]{:S(2)}) %collective-permute-start.1) | collective-permute-done | bytes 204832 | tf_op jit(solution)/shard_map/ppermute | solution.py:351
  20.7 0.9 constant_dynamic-slice_fusion
  21.5 2.0 %collective-permute-start.6 = (f32[16,5248]{1,0:T(8,128)S(1)}, f32[16,5248]{1,0:T(8,128)S(1)}, u32[]{:S(2)}, u32[]{:S(2)}) collective-permute-start(f32[16,5248]{1,0:T(8,128)S(1)} %get-tuple-element.32), channel_id=1, source_target_pairs={{0,3},{1,0},{2,1},{3,2},{4,7},{5,4},{6,5},{7,6},{8,11},{9,8},{10,9... | collective-permute-start | bytes 1007624 | tf_op jit(solution)/shard_map/ppermute | solution.py:351
  23.5 0.9 collective-permute-start.5
  24.6 15.8 %gram_first.1 = (f32[64,3200]{1,0:T(8,128)S(1)}, f32[1024,1024]{1,0:T(8,128)S(1)}) custom-call(s32[2]{0:T(128)S(1)} %pad_add_fusion.1.place_ref, f32[16,32768]{1,0:T(8,128)} %p0_ref.1, f32[16,3200]{1,0:T(8,128)} %copy-done.3, f32[16,3200]{1,0:T(8,128)} %copy-done.4, f32[16,3200]{1,0:T(8,128)} %copy-done.5), custom_call_target="tpu_custom_call" | custom-call | tf_op jit(solution)/shard_map/gram_first/pallas_call | solution.py:149
  40.5 1.5 collective-permute-done.4.p1_ref
  42.0 0.7 copy-done.2
  42.7 23.1 %gram_last.1 = (f32[64,8320]{1,0:T(8,128)S(1)}, f32[64,40,128]{2,1,0:T(8,128)S(1)}, f32[64,40,128]{2,1,0:T(8,128)S(1)}) custom-call(s32[2]{0:T(128)S(1)} %pad_add_fusion.1.place_ref, f32[16,5248]{1,0:T(8,128)} %get-tuple-element.35.p0_ref, f32[16,5248]{1,0:T(8,128)} %copy-done.2, f32[16,5248]{1,0:T(8,128)} %copy-done.1, f32[16,5248]{1,0:T(8,128)} %copy-done, ...), custom_call_target="tpu_custom_call" | custom-call | tf_op jit(solution)/shard_map/gram_last/pallas_call | solution.py:149
  65.8 0.8 collective-permute-start.7
  66.6 2.7 %collective-permute-done.7 = f32[64,40,128]{2,1,0:T(8,128)S(1)} collective-permute-done((f32[64,40,128]{2,1,0:T(8,128)S(1)}, f32[64,40,128]{2,1,0:T(8,128)S(1)}, u32[]{:S(2)}, u32[]{:S(2)}) %collective-permute-start.7) | collective-permute-done | bytes 1310752 | tf_op jit(solution)/shard_map/ppermute | solution.py:372
  69.4 29.0 %all_to_all.10 = f32[64,40,128]{2,1,0:T(8,128)S(1)} all-to-all(f32[64,40,128]{2,1,0:T(8,128)S(1)} %add.102), channel_id=1, replica_groups=mesh['x'=4,'y'=4,'core'=2,'chan'=4] {'x','y','chan'}, dimensions={0} | all-to-all | bytes 2621440 | tf_op jit(solution)/shard_map/all_to_all | solution.py:373
  98.6 24.2 %all_to_all.11.own_ref = f32[64,40,128]{2,1,0:T(8,128)S(1)} all-to-all(f32[64,40,128]{2,1,0:T(8,128)S(1)} %broadcast_in_dim.2), channel_id=1, replica_groups=mesh['x'=4,'y'=4,'core'=2,'chan'=4] {'x','y','chan'}, dimensions={0} | all-to-all | bytes 2621440 | tf_op jit(solution)/shard_map/all_to_all | solution.py:375
  122.8 3.6 %collective-permute-start.8 = (f32[64,40,128]{2,1,0:T(8,128)S(1)}, f32[64,40,128]{2,1,0:T(8,128)}, u32[]{:S(2)}, u32[]{:S(2)}) collective-permute-start(f32[64,40,128]{2,1,0:T(8,128)S(1)} %all_to_all.11.own_ref), channel_id=1, source_target_pairs={{0,4},{4,0},{1,5},{5,1},{2,6},{6,2},{3,7},{7,3},{8,12},{12,8},{9,1... | collective-permute-start | bytes 3932168 | tf_op jit(solution)/shard_map/ppermute | solution.py:376
  126.5 2.7 %collective-permute-done.8.other_ref = f32[64,40,128]{2,1,0:T(8,128)} collective-permute-done((f32[64,40,128]{2,1,0:T(8,128)S(1)}, f32[64,40,128]{2,1,0:T(8,128)}, u32[]{:S(2)}, u32[]{:S(2)}) %collective-permute-start.8) | collective-permute-done | bytes 1310752 | tf_op jit(solution)/shard_map/ppermute | solution.py:376
  129.2 46.1 %factor.1 = (f32[8,1024]{1,0:T(8,128)}, f32[128,512]{1,0:T(8,128)S(1)}) custom-call(s32[2]{0:T(128)S(1)} %pad_add_fusion.place_ref, f32[64,40,128]{2,1,0:T(8,128)S(1)} %all_to_all.11.own_ref, f32[64,40,128]{2,1,0:T(8,128)} %collective-permute-done.8.other_ref, f32[512,128]{1,0:T(8,128)} %given_ref.1), custom_call_target="tpu_custom_call" | custom-call | tf_op jit(solution)/shard_map/factor/pallas_call | solution.py:284
  175.3 7.6 %states.1 = f32[128,8192]{1,0:T(8,128)} custom-call(f32[128,512]{1,0:T(8,128)S(1)} %get-tuple-element.30.basis_ref, f32[64,8320]{1,0:T(8,128)S(1)} %get-tuple-element.31.x_ref), custom_call_target="tpu_custom_call" | custom-call | tf_op jit(solution)/shard_map/states/pallas_call | solution.py:325
  (21 shorter events, 0.6 us)
Async XLA Ops:
  2.5 9.2 %collective-permute-start.3 = (f32[16,128]{1,0:T(8,128)S(1)}, f32[16,128]{1,0:T(8,128)S(1)}, u32[]{:S(2)}, u32[]{:S(2)}) collective-permute-start(f32[16,128]{1,0:T(8,128)S(1)} %slice.3), channel_id=1, source_target_pairs={{4,0},{8,4},{12,8},{16,12},{20,16},{24,20},{28,24},{32,28},{36,32}... | collective-permute-start | bytes 24584 | tf_op jit(solution)/shard_map/ppermute | solution.py:364
  5.9 8.8 %collective-permute-start = (f32[16,3200]{1,0:T(8,128)S(1)}, f32[16,3200]{1,0:T(8,128)S(1)}, u32[]{:S(2)}, u32[]{:S(2)}) collective-permute-start(f32[16,3200]{1,0:T(8,128)S(1)} %get-tuple-element.17), channel_id=1, source_target_pairs={{0,1},{1,2},{2,3},{3,0},{4,5},{5,6},{6,7},{7,4},{8,9},{9,10},{10,1... | collective-permute-start | bytes 614408 | tf_op jit(solution)/shard_map/ppermute | solution.py:351
  7.7 13.0 %collective-permute-start.1 = (f32[16,3200]{1,0:T(8,128)S(1)}, f32[16,3200]{1,0:T(8,128)S(1)}, u32[]{:S(2)}, u32[]{:S(2)}) collective-permute-start(f32[16,3200]{1,0:T(8,128)S(1)} %get-tuple-element.18), channel_id=1, source_target_pairs={{0,2},{1,3},{2,0},{3,1},{4,6},{5,7},{6,4},{7,5},{8,10},{9,11},{10,... | collective-permute-start | bytes 614408 | tf_op jit(solution)/shard_map/ppermute | solution.py:351
  11.0 9.7 %collective-permute-start.2 = (f32[16,3200]{1,0:T(8,128)S(1)}, f32[16,3200]{1,0:T(8,128)S(1)}, u32[]{:S(2)}, u32[]{:S(2)}) collective-permute-start(f32[16,3200]{1,0:T(8,128)S(1)} %get-tuple-element.19), channel_id=1, source_target_pairs={{0,3},{1,0},{2,1},{3,2},{4,7},{5,4},{6,5},{7,6},{8,11},{9,8},{10,9... | collective-permute-start | bytes 614408 | tf_op jit(solution)/shard_map/ppermute | solution.py:351
  14.7 9.9 %copy-start.3 = (f32[16,3200]{1,0:T(8,128)}, f32[16,3200]{1,0:T(8,128)S(1)}, u32[]{:S(2)}) copy-start(f32[16,3200]{1,0:T(8,128)S(1)} %collective-permute-done.p1_ref) | copy-start | bytes 614404
  20.7 3.9 %copy-start.4 = (f32[16,3200]{1,0:T(8,128)}, f32[16,3200]{1,0:T(8,128)S(1)}, u32[]{:S(2)}) copy-start(f32[16,3200]{1,0:T(8,128)S(1)} %collective-permute-done.1.p2_ref) | copy-start | bytes 614404
  20.7 3.9 %copy-start.5 = (f32[16,3200]{1,0:T(8,128)}, f32[16,3200]{1,0:T(8,128)S(1)}, u32[]{:S(2)}) copy-start(f32[16,3200]{1,0:T(8,128)S(1)} %collective-permute-done.2.p3_ref) | copy-start | bytes 614404
  21.5 18.9 %collective-permute-start.6 = (f32[16,5248]{1,0:T(8,128)S(1)}, f32[16,5248]{1,0:T(8,128)S(1)}, u32[]{:S(2)}, u32[]{:S(2)}) collective-permute-start(f32[16,5248]{1,0:T(8,128)S(1)} %get-tuple-element.32), channel_id=1, source_target_pairs={{0,3},{1,0},{2,1},{3,2},{4,7},{5,4},{6,5},{7,6},{8,11},{9,8},{10,9... | collective-permute-start | bytes 1007624 | tf_op jit(solution)/shard_map/ppermute | solution.py:351
  23.5 16.9 %collective-permute-start.5 = (f32[16,5248]{1,0:T(8,128)S(1)}, f32[16,5248]{1,0:T(8,128)S(1)}, u32[]{:S(2)}, u32[]{:S(2)}) collective-permute-start(f32[16,5248]{1,0:T(8,128)S(1)} %get-tuple-element.33), channel_id=1, source_target_pairs={{0,2},{1,3},{2,0},{3,1},{4,6},{5,7},{6,4},{7,5},{8,10},{9,11},{10,... | collective-permute-start | bytes 1007624 | tf_op jit(solution)/shard_map/ppermute | solution.py:351
  24.4 17.6 %collective-permute-start.4 = (f32[16,5248]{1,0:T(8,128)S(1)}, f32[16,5248]{1,0:T(8,128)S(1)}, u32[]{:S(2)}, u32[]{:S(2)}) collective-permute-start(f32[16,5248]{1,0:T(8,128)S(1)} %get-tuple-element.34), channel_id=1, source_target_pairs={{0,1},{1,2},{2,3},{3,0},{4,5},{5,6},{6,7},{7,4},{8,9},{9,10},{10,1... | collective-permute-start | bytes 1007624 | tf_op jit(solution)/shard_map/ppermute | solution.py:351
  40.4 1.6 copy-start
  40.5 1.6 copy-start.1
  42.0 0.7 copy-start.2
  65.8 3.4 %collective-permute-start.7 = (f32[64,40,128]{2,1,0:T(8,128)S(1)}, f32[64,40,128]{2,1,0:T(8,128)S(1)}, u32[]{:S(2)}, u32[]{:S(2)}) collective-permute-start(f32[64,40,128]{2,1,0:T(8,128)S(1)} %get-tuple-element.28), channel_id=1, source_target_pairs={{0,4},{4,0},{1,5},{5,1},{2,6},{6,2},{3,7},{7,3},{8,12},{12,8},{9,1... | collective-permute-start | bytes 3932168 | tf_op jit(solution)/shard_map/ppermute | solution.py:372
  122.8 6.3 %collective-permute-start.8 = (f32[64,40,128]{2,1,0:T(8,128)S(1)}, f32[64,40,128]{2,1,0:T(8,128)}, u32[]{:S(2)}, u32[]{:S(2)}) collective-permute-start(f32[64,40,128]{2,1,0:T(8,128)S(1)} %all_to_all.11.own_ref), channel_id=1, source_target_pairs={{0,4},{4,0},{1,5},{5,1},{2,6},{6,2},{3,7},{7,3},{8,12},{12,8},{9,1... | collective-permute-start | bytes 3932168 | tf_op jit(solution)/shard_map/ppermute | solution.py:376

commit v4 on v3

--- a/solution.py
+++ b/solution.py
@@ -17,7 +17,8 @@
 BLOCK = 256
 PAD = 128
 STEP = 512
-CHUNK = 3072
+CHUNK = 2048
+EARLY = 1664
 TILES = 640
 F32 = jnp.float32
 BF16 = jnp.bfloat16
@@ -56,22 +57,37 @@
 
 
 def gram_kernel(size, start, place_ref, p0_ref, p1_ref, p2_ref, p3_ref, *refs):
+    group = CH // 4
+    pieces = (p0_ref, p1_ref, p2_ref, p3_ref)
+    strips = [
+        pl.ds(pl.multiple_of((place_ref[0] + 4 - away) % 4 * group, group), group) for away in range(4)
+    ]
+    bulk = []
     if start is None:
-        x_ref, g, h0, l0, h1, l1, cross, sems = refs
+        x_ref, g, cross, h0, l0, h1, l1 = refs
         base = 0
-        first = pl.multiple_of(place_ref[0] * (p0_ref.shape[1] // 4), 128)
-        p0_ref = p0_ref.at[:, pl.ds(first, size + PAD)]
+        g[...] = jnp.zeros_like(g)
+        cross[...] = jnp.zeros_like(cross)
+        for strip, piece in zip(strips, pieces):
+            x_ref[strip, :] = piece[...]
     else:
-        before_ref, sofar_ref, x_ref, keep_ref, send_ref, h0, l0, h1, l1, g, cross, sems = refs
+        before_ref, sofar_ref, mixed_ref, *refs = refs
+        x_ref, keep_ref, send_ref, h0, l0, h1, l1, g, cross, sems = refs
         base = start
-    group = CH // 4
-    copies = []
-    for away, piece in enumerate((p0_ref, p1_ref, p2_ref, p3_ref)):
-        owner = (place_ref[0] + 4 - away) % 4
-        to = x_ref.at[pl.ds(pl.multiple_of(owner * group, group), group), pl.ds(base, size + PAD)]
-        copies.append(pltpu.make_async_copy(piece, to, sems.at[away]))
-    for copy in copies:
-        copy.start()
+        early = []
+        for part, first, count, into in ((0, 0, EARLY, early), (1, EARLY, size + PAD - EARLY, bulk)):
+            for away, (strip, piece) in enumerate(zip(strips, pieces)):
+                to = x_ref.at[strip, pl.ds(base + first, count)]
+                into.append(
+                    pltpu.make_async_copy(piece.at[:, pl.ds(first, count)], to, sems.at[part, away])
+                )
+        for copy in early + bulk:
+            copy.start()
+        g[...] = sofar_ref[...]
+        cross[...] = mixed_ref[...]
+        x_ref[:, :start] = before_ref[:, :start]
+        for copy in early:
+            copy.wait()
 
     def prepare(at, high_ref, low_ref):
         window = x_ref[:, pl.ds(at, STEP + PAD)]
@@ -95,18 +111,17 @@
                 other = mul(low_ref[rows, :], high_ref[rest, :], NT)
                 g[rows, rest] += both[:, BLOCK:] + mixed[:, BLOCK:] + other
 
-    cross[...] = jnp.zeros_like(cross)
-    if start is None:
-        g[...] = jnp.zeros_like(g)
-    else:
-        g[...] = sofar_ref[...]
-        x_ref[:, :start] = before_ref[:, :start]
-    for copy in copies:
-        copy.wait()
     prepare(base, h0, l0)
 
     def pair(j, carry):
         at = base + j * (2 * STEP)
+        if bulk:
+
+            @pl.when(j == 1)
+            def _():
+                for copy in bulk:
+                    copy.wait()
+
         prepare(pl.multiple_of(at + STEP, STEP), h1, l1)
         accumulate(h0, l0)
         after = jnp.minimum(at + 2 * STEP, base + size - STEP)
@@ -115,11 +130,11 @@
         return carry
 
     lax.fori_loop(0, size // (2 * STEP), pair, 0)
+    if start is None:
+        return
     for index, top in enumerate(range(0, ORDER, BLOCK)):
         rows = slice(top, top + BLOCK)
         g[rows, rows] += cross[index] + cross[index].T
-    if start is None:
-        return
     scale = 1.0 / ((base + size) * 128)
     for core in range(2):
 
@@ -139,21 +154,22 @@
 def gram_chunk(place, pieces, before=None):
     size = pieces[1].shape[1] - PAD
     slab = pltpu.VMEM((ORDER, STEP), BF16)
-    gram = jax.ShapeDtypeStruct((ORDER, ORDER), F32)
+    square, blocks = (ORDER, ORDER), (ORDER // BLOCK, BLOCK, BLOCK)
+    gram, mixed = jax.ShapeDtypeStruct(square, F32), jax.ShapeDtypeStruct(blocks, F32)
     half = jax.ShapeDtypeStruct((64, 8 * TILES // 128, 128), F32)
-    start = None if before is None else before[0].shape[1] - PAD
-    given = [] if before is None else list(before)
-    pieces = [pltpu.with_memory_space_constraint(piece, pltpu.HBM) for piece in pieces]
+    if before is None:
+        start, given, into, out, scratch = None, [], VMEM, (gram, mixed), []
+    else:
+        start, given, into, out = before[0].shape[1] - PAD, list(before), HBM, (half, half)
+        pieces = [pltpu.with_memory_space_constraint(piece, pltpu.HBM) for piece in pieces]
+        scratch = [pltpu.VMEM(square, F32), pltpu.VMEM(blocks, F32), pltpu.SemaphoreType.DMA((2, 4))]
     x = jax.ShapeDtypeStruct((CH, size + PAD + (start or 0)), F32)
-    out = (x, gram) if start is None else (x, half, half)
     return pl.pallas_call(
         functools.partial(gram_kernel, size, start),
-        out_shape=out,
-        in_specs=[SMEM] + [HBM] * 4 + [VMEM] * len(given),
-        out_specs=(VMEM,) * len(out),
-        scratch_shapes=[slab] * 4
-        + ([] if start is None else [pltpu.VMEM((ORDER, ORDER), F32)])
-        + [pltpu.VMEM((ORDER // BLOCK, BLOCK, BLOCK), F32), pltpu.SemaphoreType.DMA((4,))],
+        out_shape=(x,) + out,
+        in_specs=[SMEM] + [into] * 4 + [VMEM] * len(given),
+        out_specs=(VMEM,) * 3,
+        scratch_shapes=[slab] * 4 + scratch,
         compiler_params=params(32),
         name="gram_first" if start is None else "gram_last",
     )(place, *pieces, *given)
@@ -337,12 +353,19 @@
     )(basis, x)
 
 
-def windows(array, starts, width, nearest):
+def windows(samples, halo, first, width, nearest):
     chans, chan = lax.axis_size("chan"), lax.axis_index("chan")
-    return [
-        lax.dynamic_slice_in_dim(array, starts((chan + away) % chans), width, 1)
-        for away in range(nearest, chans)
-    ]
+    count = samples.shape[1] // chans
+    owed = []
+    for away in range(nearest, chans):
+        to = (chan + away) % chans
+        window = lax.dynamic_slice_in_dim(samples, to * count + first, width, 1)
+        if halo is not None:
+            end = jnp.minimum((to + 1) * count, samples.shape[1] - PAD)
+            tail = lax.dynamic_slice_in_dim(samples, end, PAD, 1)
+            window = jnp.concatenate([window, jnp.where(to == chans - 1, halo, tail)], 1)
+        owed.append(window)
+    return owed
 
 
 def exchange(owed):
@@ -358,16 +381,13 @@
     count = samples.shape[1] // chans
     core = lax.axis_index("core")
     place = jnp.stack([lax.axis_index("chan"), core]).astype(jnp.int32)
-    owed = windows(samples, lambda to: to * count, CHUNK + PAD, 1)
-    owed, head = lax.optimization_barrier((owed, samples[:, :PAD]))
-    arrived = exchange(owed)
-    halo = lax.ppermute(head, TIME, [(i, i - 1) for i in range(1, times)])
-    extended = jnp.concatenate([samples, halo], 1)
-    arrived, extended = lax.optimization_barrier((arrived, extended))
-    own, *owed = windows(extended, lambda to: to * count + CHUNK, count - CHUNK + PAD, 0)
+    halo = lax.ppermute(samples[:, :PAD], TIME, [(i, i - 1) for i in range(1, times)])
+    own, *owed = windows(samples, None, 0, CHUNK + PAD, 0)
+    pieces = [own] + exchange(owed)
+    own, *owed = windows(samples, halo, CHUNK, count - CHUNK, 0)
     others = [own] + exchange(owed)
-    first, sofar = gram_chunk(place, [samples] + arrived)
-    x, keep, send = gram_chunk(place, others, (first, sofar))
+    before = gram_chunk(place, pieces)
+    x, keep, send = gram_chunk(place, others, before)
     swap = [(0, 1), (1, 0)]
     half = keep + lax.ppermute(send, "core", swap)
     half = lax.all_to_all(half, CHIPS, 0, 0, tiled=True)

time: 183 us -> 180 us (0.984)
  transfers between devices with their start and end apart: 9 -> 9, of which waited for: 5 -> 4; matrix products, arithmetic and copies ran while one was open for 1% -> 2% of each run, Pallas kernels for 9% -> 6%
where the time goes in v4:
time: 180 us
  Pallas kernels  90.9 us (50%)
  blocking collectives  51.7 us (29%)
  starting transfers between devices  17.4 us (10%)
  waiting for transfers between devices  12.5 us (7%)
  local copies, waits for them, and re-layouts  4.46 us (2%)
  other arithmetic  2.11 us (1%)
    all_to_all x2, blocking collectives, per_device(): half = lax.all_to_all(half, CHIPS, 0, 0, tiled=True)  51.7 us
    pallas_call x1, Pallas kernels, factor_and_basis(): pl.pallas_call(factor_kernel, grid=(ORDER // PANEL,), out_shape=(jax.Shap...  46.1 us
    pallas_call x2, Pallas kernels, gram_chunk(): pl.pallas_call(functools.partial(gram_kernel, size, start), out_shape=(x,...  37.1 us
    ppermute x6, starting transfers between devices, exchange(): lax.ppermute(window, 'chan', [(i, (i + away) % chans) for i in range(chan...  9.97 us
    pallas_call x1, Pallas kernels, project(): pl.pallas_call(states_kernel, grid=(count // span,), out_shape=jax.ShapeD...  7.62 us
    ppermute x6, waiting for transfers between devices, exchange(): lax.ppermute(window, 'chan', [(i, (i + away) % chans) for i in range(chan...  7.08 us
  transfers between devices with their start and end apart: 9, of which 4 were waited for; matrix products, arithmetic and copies ran while one was open for 2% of the time, Pallas kernels for 6%

profile of v4, /device:TPU:1, one launch (start us, length us, event | category | flops | bytes accessed | tf_op | source)
XLA Modules:
  0.0 179.8 jit_solution(88107533940998314)
XLA Ops:
  0.6 0.7 slice.3
  1.3 3.3 %collective-permute-start = (f32[16,128]{1,0:T(8,128)S(1)}, f32[16,128]{1,0:T(8,128)S(1)}, u32[]{:S(2)}, u32[]{:S(2)}) collective-permute-start(f32[16,128]{1,0:T(8,128)S(1)} %slice.3), channel_id=1, source_target_pairs={{4,0},{8,4},{12,8},{16,12},{20,16},{24,20},{28,24},{32,28},{36,32}... | collective-permute-start | bytes 24584 | tf_op jit(solution)/shard_map/ppermute | solution.py:384
  4.7 1.2 constant_dynamic-slice_fusion
  5.9 3.9 %collective-permute-start.6 = (f32[16,2176]{1,0:T(8,128)S(1)}, f32[16,2176]{1,0:T(8,128)S(1)}, u32[]{:S(2)}, u32[]{:S(2)}) collective-permute-start(f32[16,2176]{1,0:T(8,128)S(1)} %get-tuple-element.22), channel_id=1, source_target_pairs={{0,3},{1,0},{2,1},{3,2},{4,7},{5,4},{6,5},{7,6},{8,11},{9,8},{10,9... | collective-permute-start | bytes 417800 | tf_op jit(solution)/shard_map/ppermute | solution.py:374
  9.8 1.3 collective-permute-start.5
  11.1 1.5 constant_dynamic-slice_fusion.4
  12.6 0.9 dynamic-slice_select_fusion
  13.5 2.0 %collective-permute-start.1 = (f32[16,6272]{1,0:T(8,128)S(1)}, f32[16,6272]{1,0:T(8,128)S(1)}, u32[]{:S(2)}, u32[]{:S(2)}) collective-permute-start(f32[16,6272]{1,0:T(8,128)S(1)} %pad_maximum_fusion.1), channel_id=1, source_target_pairs={{0,1},{1,2},{2,3},{3,0},{4,5},{5,6},{6,7},{7,4},{8,9},{9,10},{10,1... | collective-permute-start | bytes 1204232 | tf_op jit(solution)/shard_map/ppermute | solution.py:374
  15.6 0.7 collective-permute-start.2
  16.3 2.1 %collective-permute-start.3 = (f32[16,6272]{1,0:T(8,128)S(1)}, f32[16,6272]{1,0:T(8,128)S(1)}, u32[]{:S(2)}, u32[]{:S(2)}) collective-permute-start(f32[16,6272]{1,0:T(8,128)S(1)} %pad_maximum_fusion.3), channel_id=1, source_target_pairs={{0,3},{1,0},{2,1},{3,2},{4,7},{5,4},{6,5},{7,6},{8,11},{9,8},{10,9... | collective-permute-start | bytes 1204232 | tf_op jit(solution)/shard_map/ppermute | solution.py:374
  18.4 0.8 pad_maximum_fusion.p0_ref
  19.1 0.4 collective-permute-done.4.p1_ref
  19.6 10.5 %gram_first.1 = (f32[64,2176]{1,0:T(8,128)S(1)}, f32[1024,1024]{1,0:T(8,128)S(1)}, f32[4,256,256]{2,1,0:T(8,128)S(1)}) custom-call(s32[2]{0:T(128)S(1)} %pad_add_fusion.1.place_ref, f32[16,2176]{1,0:T(8,128)S(1)} %get-tuple-element.24.p0_ref, f32[16,2176]{1,0:T(8,128)S(1)} %collective-permute-done.4.p1_ref, f32[16,2176]{1,0:T(8,128)S(1)} %collective-permute-done.5.p2_ref, ...), custom_call_target="tpu_custom_call" | custom-call | tf_op jit(solution)/shard_map/gram_first/pallas_call | solution.py:167
  30.1 6.7 %collective-permute-done.1.p1_ref = f32[16,6272]{1,0:T(8,128)S(1)} collective-permute-done((f32[16,6272]{1,0:T(8,128)S(1)}, f32[16,6272]{1,0:T(8,128)S(1)}, u32[]{:S(2)}, u32[]{:S(2)}) %collective-permute-start.1) | collective-permute-done | bytes 401440 | tf_op jit(solution)/shard_map/ppermute | solution.py:374
  36.8 0.7 copy-done
  37.8 26.6 %gram_last.1 = (f32[64,8320]{1,0:T(8,128)S(1)}, f32[64,40,128]{2,1,0:T(8,128)S(1)}, f32[64,40,128]{2,1,0:T(8,128)S(1)}) custom-call(s32[2]{0:T(128)S(1)} %pad_add_fusion.1.place_ref, f32[16,6272]{1,0:T(8,128)} %pad_maximum_fusion.p0_ref, f32[16,6272]{1,0:T(8,128)} %copy-done, f32[16,6272]{1,0:T(8,128)} %copy-done.1, f32[16,6272]{1,0:T(8,128)} %copy-done.2, ...), custom_call_target="tpu_custom_call" | custom-call | tf_op jit(solution)/shard_map/gram_last/pallas_call | solution.py:167
  64.5 0.6 collective-permute-start.7
  65.0 2.7 %collective-permute-done.7 = f32[64,40,128]{2,1,0:T(8,128)S(1)} collective-permute-done((f32[64,40,128]{2,1,0:T(8,128)S(1)}, f32[64,40,128]{2,1,0:T(8,128)S(1)}, u32[]{:S(2)}, u32[]{:S(2)}) %collective-permute-start.7) | collective-permute-done | bytes 1310752 | tf_op jit(solution)/shard_map/ppermute | solution.py:392
  67.8 27.4 %all_to_all.10 = f32[64,40,128]{2,1,0:T(8,128)S(1)} all-to-all(f32[64,40,128]{2,1,0:T(8,128)S(1)} %add.139), channel_id=1, replica_groups=mesh['x'=4,'y'=4,'core'=2,'chan'=4] {'x','y','chan'}, dimensions={0} | all-to-all | bytes 2621440 | tf_op jit(solution)/shard_map/all_to_all | solution.py:393
  95.5 24.2 %all_to_all.11.own_ref = f32[64,40,128]{2,1,0:T(8,128)S(1)} all-to-all(f32[64,40,128]{2,1,0:T(8,128)S(1)} %broadcast_in_dim.2), channel_id=1, replica_groups=mesh['x'=4,'y'=4,'core'=2,'chan'=4] {'x','y','chan'}, dimensions={0} | all-to-all | bytes 2621440 | tf_op jit(solution)/shard_map/all_to_all | solution.py:395
  119.7 3.6 %collective-permute-start.8 = (f32[64,40,128]{2,1,0:T(8,128)S(1)}, f32[64,40,128]{2,1,0:T(8,128)}, u32[]{:S(2)}, u32[]{:S(2)}) collective-permute-start(f32[64,40,128]{2,1,0:T(8,128)S(1)} %all_to_all.11.own_ref), channel_id=1, source_target_pairs={{0,4},{4,0},{1,5},{5,1},{2,6},{6,2},{3,7},{7,3},{8,12},{12,8},{9,1... | collective-permute-start | bytes 3932168 | tf_op jit(solution)/shard_map/ppermute | solution.py:396
  123.4 2.7 %collective-permute-done.8.other_ref = f32[64,40,128]{2,1,0:T(8,128)} collective-permute-done((f32[64,40,128]{2,1,0:T(8,128)S(1)}, f32[64,40,128]{2,1,0:T(8,128)}, u32[]{:S(2)}, u32[]{:S(2)}) %collective-permute-start.8) | collective-permute-done | bytes 1310752 | tf_op jit(solution)/shard_map/ppermute | solution.py:396
  126.1 46.1 %factor.1 = (f32[8,1024]{1,0:T(8,128)}, f32[128,512]{1,0:T(8,128)S(1)}) custom-call(s32[2]{0:T(128)S(1)} %pad_add_fusion.place_ref, f32[64,40,128]{2,1,0:T(8,128)S(1)} %all_to_all.11.own_ref, f32[64,40,128]{2,1,0:T(8,128)} %collective-permute-done.8.other_ref, f32[512,128]{1,0:T(8,128)} %given_ref.1), custom_call_target="tpu_custom_call" | custom-call | tf_op jit(solution)/shard_map/factor/pallas_call | solution.py:300
  172.2 7.6 %states.1 = f32[128,8192]{1,0:T(8,128)} custom-call(f32[128,512]{1,0:T(8,128)S(1)} %get-tuple-element.16.basis_ref, f32[64,8320]{1,0:T(8,128)S(1)} %get-tuple-element.17.x_ref), custom_call_target="tpu_custom_call" | custom-call | tf_op jit(solution)/shard_map/states/pallas_call | solution.py:341
  (19 shorter events, 0.9 us)
Async XLA Ops:
  1.3 11.3 %collective-permute-start = (f32[16,128]{1,0:T(8,128)S(1)}, f32[16,128]{1,0:T(8,128)S(1)}, u32[]{:S(2)}, u32[]{:S(2)}) collective-permute-start(f32[16,128]{1,0:T(8,128)S(1)} %slice.3), channel_id=1, source_target_pairs={{4,0},{8,4},{12,8},{16,12},{20,16},{24,20},{28,24},{32,28},{36,32}... | collective-permute-start | bytes 24584 | tf_op jit(solution)/shard_map/ppermute | solution.py:384
  5.9 10.4 %collective-permute-start.6 = (f32[16,2176]{1,0:T(8,128)S(1)}, f32[16,2176]{1,0:T(8,128)S(1)}, u32[]{:S(2)}, u32[]{:S(2)}) collective-permute-start(f32[16,2176]{1,0:T(8,128)S(1)} %get-tuple-element.22), channel_id=1, source_target_pairs={{0,3},{1,0},{2,1},{3,2},{4,7},{5,4},{6,5},{7,6},{8,11},{9,8},{10,9... | collective-permute-start | bytes 417800 | tf_op jit(solution)/shard_map/ppermute | solution.py:374
  9.8 9.8 %collective-permute-start.4 = (f32[16,2176]{1,0:T(8,128)S(1)}, f32[16,2176]{1,0:T(8,128)S(1)}, u32[]{:S(2)}, u32[]{:S(2)}) collective-permute-start(f32[16,2176]{1,0:T(8,128)S(1)} %get-tuple-element.23), channel_id=1, source_target_pairs={{0,1},{1,2},{2,3},{3,0},{4,5},{5,6},{6,7},{7,4},{8,9},{9,10},{10,1... | collective-permute-start | bytes 417800 | tf_op jit(solution)/shard_map/ppermute | solution.py:374
  9.8 9.8 %collective-permute-start.5 = (f32[16,2176]{1,0:T(8,128)S(1)}, f32[16,2176]{1,0:T(8,128)S(1)}, u32[]{:S(2)}, u32[]{:S(2)}) collective-permute-start(f32[16,2176]{1,0:T(8,128)S(1)} %get-tuple-element.25), channel_id=1, source_target_pairs={{0,2},{1,3},{2,0},{3,1},{4,6},{5,7},{6,4},{7,5},{8,10},{9,11},{10,... | collective-permute-start | bytes 417800 | tf_op jit(solution)/shard_map/ppermute | solution.py:374
  13.5 23.2 %collective-permute-start.1 = (f32[16,6272]{1,0:T(8,128)S(1)}, f32[16,6272]{1,0:T(8,128)S(1)}, u32[]{:S(2)}, u32[]{:S(2)}) collective-permute-start(f32[16,6272]{1,0:T(8,128)S(1)} %pad_maximum_fusion.1), channel_id=1, source_target_pairs={{0,1},{1,2},{2,3},{3,0},{4,5},{5,6},{6,7},{7,4},{8,9},{9,10},{10,1... | collective-permute-start | bytes 1204232 | tf_op jit(solution)/shard_map/ppermute | solution.py:374
  15.6 21.2 %collective-permute-start.2 = (f32[16,6272]{1,0:T(8,128)S(1)}, f32[16,6272]{1,0:T(8,128)S(1)}, u32[]{:S(2)}, u32[]{:S(2)}) collective-permute-start(f32[16,6272]{1,0:T(8,128)S(1)} %pad_maximum_fusion.2), channel_id=1, source_target_pairs={{0,2},{1,3},{2,0},{3,1},{4,6},{5,7},{6,4},{7,5},{8,10},{9,11},{10,... | collective-permute-start | bytes 1204232 | tf_op jit(solution)/shard_map/ppermute | solution.py:374
  16.3 20.5 %collective-permute-start.3 = (f32[16,6272]{1,0:T(8,128)S(1)}, f32[16,6272]{1,0:T(8,128)S(1)}, u32[]{:S(2)}, u32[]{:S(2)}) collective-permute-start(f32[16,6272]{1,0:T(8,128)S(1)} %pad_maximum_fusion.3), channel_id=1, source_target_pairs={{0,3},{1,0},{2,1},{3,2},{4,7},{5,4},{6,5},{7,6},{8,11},{9,8},{10,9... | collective-permute-start | bytes 1204232 | tf_op jit(solution)/shard_map/ppermute | solution.py:374
  36.8 0.7 copy-start
  36.8 0.9 copy-start.1
  36.8 1.1 copy-start.2
  64.5 3.3 %collective-permute-start.7 = (f32[64,40,128]{2,1,0:T(8,128)S(1)}, f32[64,40,128]{2,1,0:T(8,128)S(1)}, u32[]{:S(2)}, u32[]{:S(2)}) collective-permute-start(f32[64,40,128]{2,1,0:T(8,128)S(1)} %get-tuple-element.14), channel_id=1, source_target_pairs={{0,4},{4,0},{1,5},{5,1},{2,6},{6,2},{3,7},{7,3},{8,12},{12,8},{9,1... | collective-permute-start | bytes 3932168 | tf_op jit(solution)/shard_map/ppermute | solution.py:392
  119.7 6.4 %collective-permute-start.8 = (f32[64,40,128]{2,1,0:T(8,128)S(1)}, f32[64,40,128]{2,1,0:T(8,128)}, u32[]{:S(2)}, u32[]{:S(2)}) collective-permute-start(f32[64,40,128]{2,1,0:T(8,128)S(1)} %all_to_all.11.own_ref), channel_id=1, source_target_pairs={{0,4},{4,0},{1,5},{5,1},{2,6},{6,2},{3,7},{7,3},{8,12},{12,8},{9,1... | collective-permute-start | bytes 3932168 | tf_op jit(solution)/shard_map/ppermute | solution.py:396

commit v5 on v4

--- a/solution.py
+++ b/solution.py
@@ -17,7 +17,7 @@
 BLOCK = 256
 PAD = 128
 STEP = 512
-CHUNK = 2048
+CHUNK = 3072
 EARLY = 1664
 TILES = 640
 F32 = jnp.float32
@@ -189,10 +189,13 @@
     cols = lax.broadcasted_iota(jnp.int32, (8, 128), 1)
     w = [jnp.where(cols == rows + 8 * i, 1.0, 0.0).astype(F32) for i in range(n)]
     upper, inverse = [], []
+    cn = [lane(d[0], j) for j in range(8)]
     for g in range(n):
-        cg = [lane(d[g], 8 * g + j) for j in range(8)]
+        cg = cn
         below = range(g + 1, n)
         cb = {i: [lane(d[i], 8 * g + j) for j in range(8)] for i in below}
+        if g + 1 < n:
+            cn = [lane(d[g + 1], 8 * (g + 1) + k) for k in range(8)]
         dg, wg = d[g], w[g]
         tops, inv = [], []
         pivots = jnp.zeros((8, 128), F32)
@@ -201,13 +204,13 @@
             r = 1.0 / pivot
             inv.append(r)
             pivots = jnp.where(rows == j, pivot, pivots)
-            m = jnp.where(rows > j, cg[j] * r, 0.0)
+            under = jnp.where(rows > j, cg[j], 0.0)
             top = {k: row(cg[k], j) for k in range(j + 1, 8)}
             tops.append(top)
             for k in range(j + 1, 8):
-                cg[k] = cg[k] - m * top[k]
-            dg = dg - m * row(dg, j)
-            wg = wg - m * row(wg, j)
+                cg[k] = cg[k] - (under * top[k]) * r
+            dg = dg - (under * row(dg, j)) * r
+            wg = wg - (under * row(wg, j)) * r
         scale = lax.rsqrt(pivots)
         upper.append(jnp.where(cols >= rows + 8 * g, dg * scale, 0.0))
         inverse.append(wg * scale)
@@ -217,6 +220,8 @@
             c, di, wi = cb[i], d[i], w[i]
             for j in range(8):
                 m = c[j] * inv[j]
+                if i == g + 1:
+                    cn = [cn[k] - m * row(c[j], k) for k in range(8)]
                 for k in range(j + 1, 8):
                     c[k] = c[k] - m * tops[j][k]
                 di = di - m * ds[j]

time: 180 us -> 179 us (level)
  Pallas kernels: 90.9 us -> 85.2 us
  waiting for transfers between devices: 12.5 us -> 15.4 us
    pallas_call x1, Pallas kernels: 46.1 us -> 40.3 us  [factor_and_basis(): pl.pallas_call(factor_kernel, grid=(ORDER // PANEL,), out_shape=(jax.Shap...]
    ppermute x6, waiting for transfers between devices: 7.08 us -> 9.99 us  [exchange(): lax.ppermute(window, 'chan', [(i, (i + away) % chans) for i in range(chan...]
  transfers between devices with their start and end apart: 9 -> 9, of which waited for: 4 -> 3; matrix products, arithmetic and copies ran while one was open for 2% -> 3% of each run, Pallas kernels for 6% -> 8%
where the time goes in v5:
time: 179 us; the launch traced here: 178 us
  Pallas kernels  85.2 us (48%)
  blocking collectives  51.7 us (29%)
  starting transfers between devices  18.8 us (11%)
  waiting for transfers between devices  15.4 us (9%)
  local copies, waits for them, and re-layouts  4.38 us (2%)
  other arithmetic  2.07 us (1%)
    all_to_all x2, blocking collectives, per_device(): half = lax.all_to_all(half, CHIPS, 0, 0, tiled=True)  51.7 us
    pallas_call x1, Pallas kernels, factor_and_basis(): pl.pallas_call(factor_kernel, grid=(ORDER // PANEL,), out_shape=(jax.Shap...  40.3 us
    pallas_call x2, Pallas kernels, gram_chunk(): pl.pallas_call(functools.partial(gram_kernel, size, start), out_shape=(x,...  37.4 us
    ppermute x6, starting transfers between devices, exchange(): lax.ppermute(window, 'chan', [(i, (i + away) % chans) for i in range(chan...  11.1 us
    ppermute x6, waiting for transfers between devices, exchange(): lax.ppermute(window, 'chan', [(i, (i + away) % chans) for i in range(chan...  9.99 us
    pallas_call x1, Pallas kernels, project(): pl.pallas_call(states_kernel, grid=(count // span,), out_shape=jax.ShapeD...  7.62 us
  transfers between devices with their start and end apart: 9, of which 3 were waited for; matrix products, arithmetic and copies ran while one was open for 3% of the time, Pallas kernels for 8%

profile of v5, /device:TPU:1, one launch (start us, length us, event | category | flops | bytes accessed | tf_op | source)
XLA Modules:
  0.0 178.3 jit_solution(11982865059498169740)
XLA Ops:
  0.6 0.7 slice.3
  1.3 3.3 %collective-permute-start = (f32[16,128]{1,0:T(8,128)S(1)}, f32[16,128]{1,0:T(8,128)S(1)}, u32[]{:S(2)}, u32[]{:S(2)}) collective-permute-start(f32[16,128]{1,0:T(8,128)S(1)} %slice.3), channel_id=1, source_target_pairs={{4,0},{8,4},{12,8},{16,12},{20,16},{24,20},{28,24},{32,28},{36,32}... | collective-permute-start | bytes 24584 | tf_op jit(solution)/shard_map/ppermute | solution.py:389
  4.7 1.3 constant_dynamic-slice_fusion
  6.0 3.9 %collective-permute-start.6 = (f32[16,3200]{1,0:T(8,128)S(1)}, f32[16,3200]{1,0:T(8,128)S(1)}, u32[]{:S(2)}, u32[]{:S(2)}) collective-permute-start(f32[16,3200]{1,0:T(8,128)S(1)} %get-tuple-element.22), channel_id=1, source_target_pairs={{0,3},{1,0},{2,1},{3,2},{4,7},{5,4},{6,5},{7,6},{8,11},{9,8},{10,9... | collective-permute-start | bytes 614408 | tf_op jit(solution)/shard_map/ppermute | solution.py:379
  9.9 1.3 collective-permute-start.5
  11.2 1.4 constant_dynamic-slice_fusion.4
  12.7 0.9 dynamic-slice_select_fusion
  13.6 2.0 %collective-permute-start.1 = (f32[16,5248]{1,0:T(8,128)S(1)}, f32[16,5248]{1,0:T(8,128)S(1)}, u32[]{:S(2)}, u32[]{:S(2)}) collective-permute-start(f32[16,5248]{1,0:T(8,128)S(1)} %pad_maximum_fusion.1), channel_id=1, source_target_pairs={{0,1},{1,2},{2,3},{3,0},{4,5},{5,6},{6,7},{7,4},{8,9},{9,10},{10,1... | collective-permute-start | bytes 1007624 | tf_op jit(solution)/shard_map/ppermute | solution.py:379
  15.6 0.7 collective-permute-start.2
  16.3 10.0 %collective-permute-done.6.p3_ref = f32[16,3200]{1,0:T(8,128)S(1)} collective-permute-done((f32[16,3200]{1,0:T(8,128)S(1)}, f32[16,3200]{1,0:T(8,128)S(1)}, u32[]{:S(2)}, u32[]{:S(2)}) %collective-permute-start.6) | collective-permute-done | bytes 204832 | tf_op jit(solution)/shard_map/ppermute | solution.py:379
  26.3 3.2 %collective-permute-start.3 = (f32[16,5248]{1,0:T(8,128)S(1)}, f32[16,5248]{1,0:T(8,128)S(1)}, u32[]{:S(2)}, u32[]{:S(2)}) collective-permute-start(f32[16,5248]{1,0:T(8,128)S(1)} %pad_maximum_fusion.3), channel_id=1, source_target_pairs={{0,3},{1,0},{2,1},{3,2},{4,7},{5,4},{6,5},{7,6},{8,11},{9,8},{10,9... | collective-permute-start | bytes 1007624 | tf_op jit(solution)/shard_map/ppermute | solution.py:379
  29.5 0.8 pad_maximum_fusion.p0_ref
  30.3 14.5 %gram_first.1 = (f32[64,3200]{1,0:T(8,128)S(1)}, f32[1024,1024]{1,0:T(8,128)S(1)}, f32[4,256,256]{2,1,0:T(8,128)S(1)}) custom-call(s32[2]{0:T(128)S(1)} %pad_add_fusion.1.place_ref, f32[16,3200]{1,0:T(8,128)S(1)} %get-tuple-element.24.p0_ref, f32[16,3200]{1,0:T(8,128)S(1)} %collective-permute-done.4.p1_ref, f32[16,3200]{1,0:T(8,128)S(1)} %collective-permute-done.5.p2_ref, ...), custom_call_target="tpu_custom_call" | custom-call | tf_op jit(solution)/shard_map/gram_first/pallas_call | solution.py:167
  44.8 0.7 copy-done
  45.8 22.8 %gram_last.1 = (f32[64,8320]{1,0:T(8,128)S(1)}, f32[64,40,128]{2,1,0:T(8,128)S(1)}, f32[64,40,128]{2,1,0:T(8,128)S(1)}) custom-call(s32[2]{0:T(128)S(1)} %pad_add_fusion.1.place_ref, f32[16,5248]{1,0:T(8,128)} %pad_maximum_fusion.p0_ref, f32[16,5248]{1,0:T(8,128)} %copy-done, f32[16,5248]{1,0:T(8,128)} %copy-done.1, f32[16,5248]{1,0:T(8,128)} %copy-done.2, ...), custom_call_target="tpu_custom_call" | custom-call | tf_op jit(solution)/shard_map/gram_last/pallas_call | solution.py:167
  68.6 0.8 collective-permute-start.7
  69.4 2.7 %collective-permute-done.7 = f32[64,40,128]{2,1,0:T(8,128)S(1)} collective-permute-done((f32[64,40,128]{2,1,0:T(8,128)S(1)}, f32[64,40,128]{2,1,0:T(8,128)S(1)}, u32[]{:S(2)}, u32[]{:S(2)}) %collective-permute-start.7) | collective-permute-done | bytes 1310752 | tf_op jit(solution)/shard_map/ppermute | solution.py:397
  72.0 0.1 add.139
  72.2 27.4 %all_to_all.10 = f32[64,40,128]{2,1,0:T(8,128)S(1)} all-to-all(f32[64,40,128]{2,1,0:T(8,128)S(1)} %add.139), channel_id=1, replica_groups=mesh['x'=4,'y'=4,'core'=2,'chan'=4] {'x','y','chan'}, dimensions={0} | all-to-all | bytes 2621440 | tf_op jit(solution)/shard_map/all_to_all | solution.py:398
  99.8 24.2 %all_to_all.11.own_ref = f32[64,40,128]{2,1,0:T(8,128)S(1)} all-to-all(f32[64,40,128]{2,1,0:T(8,128)S(1)} %broadcast_in_dim.2), channel_id=1, replica_groups=mesh['x'=4,'y'=4,'core'=2,'chan'=4] {'x','y','chan'}, dimensions={0} | all-to-all | bytes 2621440 | tf_op jit(solution)/shard_map/all_to_all | solution.py:400
  124.0 3.6 %collective-permute-start.8 = (f32[64,40,128]{2,1,0:T(8,128)S(1)}, f32[64,40,128]{2,1,0:T(8,128)}, u32[]{:S(2)}, u32[]{:S(2)}) collective-permute-start(f32[64,40,128]{2,1,0:T(8,128)S(1)} %all_to_all.11.own_ref), channel_id=1, source_target_pairs={{0,4},{4,0},{1,5},{5,1},{2,6},{6,2},{3,7},{7,3},{8,12},{12,8},{9,1... | collective-permute-start | bytes 3932168 | tf_op jit(solution)/shard_map/ppermute | solution.py:401
  127.7 2.7 %collective-permute-done.8.other_ref = f32[64,40,128]{2,1,0:T(8,128)} collective-permute-done((f32[64,40,128]{2,1,0:T(8,128)S(1)}, f32[64,40,128]{2,1,0:T(8,128)}, u32[]{:S(2)}, u32[]{:S(2)}) %collective-permute-start.8) | collective-permute-done | bytes 1310752 | tf_op jit(solution)/shard_map/ppermute | solution.py:401
  130.4 40.3 %factor.1 = (f32[8,1024]{1,0:T(8,128)}, f32[128,512]{1,0:T(8,128)S(1)}) custom-call(s32[2]{0:T(128)S(1)} %pad_add_fusion.place_ref, f32[64,40,128]{2,1,0:T(8,128)S(1)} %all_to_all.11.own_ref, f32[64,40,128]{2,1,0:T(8,128)} %collective-permute-done.8.other_ref, f32[512,128]{1,0:T(8,128)} %given_ref.1), custom_call_target="tpu_custom_call" | custom-call | tf_op jit(solution)/shard_map/factor/pallas_call | solution.py:305
  170.7 7.6 %states.1 = f32[128,8192]{1,0:T(8,128)} custom-call(f32[128,512]{1,0:T(8,128)S(1)} %get-tuple-element.16.basis_ref, f32[64,8320]{1,0:T(8,128)S(1)} %get-tuple-element.17.x_ref), custom_call_target="tpu_custom_call" | custom-call | tf_op jit(solution)/shard_map/states/pallas_call | solution.py:346
  (19 shorter events, 0.7 us)
Async XLA Ops:
  1.3 11.4 %collective-permute-start = (f32[16,128]{1,0:T(8,128)S(1)}, f32[16,128]{1,0:T(8,128)S(1)}, u32[]{:S(2)}, u32[]{:S(2)}) collective-permute-start(f32[16,128]{1,0:T(8,128)S(1)} %slice.3), channel_id=1, source_target_pairs={{4,0},{8,4},{12,8},{16,12},{20,16},{24,20},{28,24},{32,28},{36,32}... | collective-permute-start | bytes 24584 | tf_op jit(solution)/shard_map/ppermute | solution.py:389
  6.0 20.3 %collective-permute-start.6 = (f32[16,3200]{1,0:T(8,128)S(1)}, f32[16,3200]{1,0:T(8,128)S(1)}, u32[]{:S(2)}, u32[]{:S(2)}) collective-permute-start(f32[16,3200]{1,0:T(8,128)S(1)} %get-tuple-element.22), channel_id=1, source_target_pairs={{0,3},{1,0},{2,1},{3,2},{4,7},{5,4},{6,5},{7,6},{8,11},{9,8},{10,9... | collective-permute-start | bytes 614408 | tf_op jit(solution)/shard_map/ppermute | solution.py:379
  9.9 20.3 %collective-permute-start.4 = (f32[16,3200]{1,0:T(8,128)S(1)}, f32[16,3200]{1,0:T(8,128)S(1)}, u32[]{:S(2)}, u32[]{:S(2)}) collective-permute-start(f32[16,3200]{1,0:T(8,128)S(1)} %get-tuple-element.23), channel_id=1, source_target_pairs={{0,1},{1,2},{2,3},{3,0},{4,5},{5,6},{6,7},{7,4},{8,9},{9,10},{10,1... | collective-permute-start | bytes 614408 | tf_op jit(solution)/shard_map/ppermute | solution.py:379
  9.9 20.3 %collective-permute-start.5 = (f32[16,3200]{1,0:T(8,128)S(1)}, f32[16,3200]{1,0:T(8,128)S(1)}, u32[]{:S(2)}, u32[]{:S(2)}) collective-permute-start(f32[16,3200]{1,0:T(8,128)S(1)} %get-tuple-element.25), channel_id=1, source_target_pairs={{0,2},{1,3},{2,0},{3,1},{4,6},{5,7},{6,4},{7,5},{8,10},{9,11},{10,... | collective-permute-start | bytes 614408 | tf_op jit(solution)/shard_map/ppermute | solution.py:379
  13.6 31.2 %collective-permute-start.1 = (f32[16,5248]{1,0:T(8,128)S(1)}, f32[16,5248]{1,0:T(8,128)S(1)}, u32[]{:S(2)}, u32[]{:S(2)}) collective-permute-start(f32[16,5248]{1,0:T(8,128)S(1)} %pad_maximum_fusion.1), channel_id=1, source_target_pairs={{0,1},{1,2},{2,3},{3,0},{4,5},{5,6},{6,7},{7,4},{8,9},{9,10},{10,1... | collective-permute-start | bytes 1007624 | tf_op jit(solution)/shard_map/ppermute | solution.py:379
  15.6 29.2 %collective-permute-start.2 = (f32[16,5248]{1,0:T(8,128)S(1)}, f32[16,5248]{1,0:T(8,128)S(1)}, u32[]{:S(2)}, u32[]{:S(2)}) collective-permute-start(f32[16,5248]{1,0:T(8,128)S(1)} %pad_maximum_fusion.2), channel_id=1, source_target_pairs={{0,2},{1,3},{2,0},{3,1},{4,6},{5,7},{6,4},{7,5},{8,10},{9,11},{10,... | collective-permute-start | bytes 1007624 | tf_op jit(solution)/shard_map/ppermute | solution.py:379
  26.3 18.5 %collective-permute-start.3 = (f32[16,5248]{1,0:T(8,128)S(1)}, f32[16,5248]{1,0:T(8,128)S(1)}, u32[]{:S(2)}, u32[]{:S(2)}) collective-permute-start(f32[16,5248]{1,0:T(8,128)S(1)} %pad_maximum_fusion.3), channel_id=1, source_target_pairs={{0,3},{1,0},{2,1},{3,2},{4,7},{5,4},{6,5},{7,6},{8,11},{9,8},{10,9... | collective-permute-start | bytes 1007624 | tf_op jit(solution)/shard_map/ppermute | solution.py:379
  44.8 0.7 copy-start
  44.8 0.8 copy-start.1
  44.8 0.9 copy-start.2
  68.6 3.4 %collective-permute-start.7 = (f32[64,40,128]{2,1,0:T(8,128)S(1)}, f32[64,40,128]{2,1,0:T(8,128)S(1)}, u32[]{:S(2)}, u32[]{:S(2)}) collective-permute-start(f32[64,40,128]{2,1,0:T(8,128)S(1)} %get-tuple-element.14), channel_id=1, source_target_pairs={{0,4},{4,0},{1,5},{5,1},{2,6},{6,2},{3,7},{7,3},{8,12},{12,8},{9,1... | collective-permute-start | bytes 3932168 | tf_op jit(solution)/shard_map/ppermute | solution.py:397
  124.0 6.4 %collective-permute-start.8 = (f32[64,40,128]{2,1,0:T(8,128)S(1)}, f32[64,40,128]{2,1,0:T(8,128)}, u32[]{:S(2)}, u32[]{:S(2)}) collective-permute-start(f32[64,40,128]{2,1,0:T(8,128)S(1)} %all_to_all.11.own_ref), channel_id=1, source_target_pairs={{0,4},{4,0},{1,5},{5,1},{2,6},{6,2},{3,7},{7,3},{8,12},{12,8},{9,1... | collective-permute-start | bytes 3932168 | tf_op jit(solution)/shard_map/ppermute | solution.py:401

commit v6 on v5

--- a/solution.py
+++ b/solution.py
@@ -17,7 +17,7 @@
 BLOCK = 256
 PAD = 128
 STEP = 512
-CHUNK = 3072
+CHUNK = 2048
 EARLY = 1664
 TILES = 640
 F32 = jnp.float32

time: 179 us -> 174 us (0.972)
  waiting for transfers between devices: 15.4 us -> 12.5 us
    ppermute x6, waiting for transfers between devices: 9.99 us -> 7.08 us  [exchange(): lax.ppermute(window, 'chan', [(i, (i + away) % chans) for i in range(chan...]
  transfers between devices with their start and end apart: 9 -> 9, of which waited for: 3 -> 4; matrix products, arithmetic and copies ran while one was open for 3% -> 3% of each run, Pallas kernels for 8% -> 6%
where the time goes in v6:
time: 174 us
  Pallas kernels  85 us (49%)
  blocking collectives  51.7 us (30%)
  starting transfers between devices  17.4 us (10%)
  waiting for transfers between devices  12.5 us (7%)
  local copies, waits for them, and re-layouts  4.46 us (3%)
  other arithmetic  2.11 us (1%)
    all_to_all x2, blocking collectives, per_device(): half = lax.all_to_all(half, CHIPS, 0, 0, tiled=True)  51.7 us
    pallas_call x1, Pallas kernels, factor_and_basis(): pl.pallas_call(factor_kernel, grid=(ORDER // PANEL,), out_shape=(jax.Shap...  40.3 us
    pallas_call x2, Pallas kernels, gram_chunk(): pl.pallas_call(functools.partial(gram_kernel, size, start), out_shape=(x,...  37.1 us
    ppermute x6, starting transfers between devices, exchange(): lax.ppermute(window, 'chan', [(i, (i + away) % chans) for i in range(chan...  9.97 us
    pallas_call x1, Pallas kernels, project(): pl.pallas_call(states_kernel, grid=(count // span,), out_shape=jax.ShapeD...  7.62 us
    ppermute x6, waiting for transfers between devices, exchange(): lax.ppermute(window, 'chan', [(i, (i + away) % chans) for i in range(chan...  7.08 us
    ppermute x1, starting transfers between devices, per_device(): other = lax.ppermute(half, 'core', swap)  3.56 us
  transfers between devices with their start and end apart: 9, of which 4 were waited for; matrix products, arithmetic and copies ran while one was open for 3% of the time, Pallas kernels for 6%

profile of v6, /device:TPU:1, one launch (start us, length us, event | category | flops | bytes accessed | tf_op | source)
XLA Modules:
  0.0 174.0 jit_solution(18321680587548714291)
XLA Ops:
  0.6 0.7 slice.3
  1.3 3.3 %collective-permute-start = (f32[16,128]{1,0:T(8,128)S(1)}, f32[16,128]{1,0:T(8,128)S(1)}, u32[]{:S(2)}, u32[]{:S(2)}) collective-permute-start(f32[16,128]{1,0:T(8,128)S(1)} %slice.3), channel_id=1, source_target_pairs={{4,0},{8,4},{12,8},{16,12},{20,16},{24,20},{28,24},{32,28},{36,32}... | collective-permute-start | bytes 24584 | tf_op jit(solution)/shard_map/ppermute | solution.py:389
  4.7 1.2 constant_dynamic-slice_fusion
  5.9 3.9 %collective-permute-start.6 = (f32[16,2176]{1,0:T(8,128)S(1)}, f32[16,2176]{1,0:T(8,128)S(1)}, u32[]{:S(2)}, u32[]{:S(2)}) collective-permute-start(f32[16,2176]{1,0:T(8,128)S(1)} %get-tuple-element.22), channel_id=1, source_target_pairs={{0,3},{1,0},{2,1},{3,2},{4,7},{5,4},{6,5},{7,6},{8,11},{9,8},{10,9... | collective-permute-start | bytes 417800 | tf_op jit(solution)/shard_map/ppermute | solution.py:379
  9.8 1.3 collective-permute-start.5
  11.1 1.5 constant_dynamic-slice_fusion.4
  12.6 0.9 dynamic-slice_select_fusion
  13.5 2.0 %collective-permute-start.1 = (f32[16,6272]{1,0:T(8,128)S(1)}, f32[16,6272]{1,0:T(8,128)S(1)}, u32[]{:S(2)}, u32[]{:S(2)}) collective-permute-start(f32[16,6272]{1,0:T(8,128)S(1)} %pad_maximum_fusion.1), channel_id=1, source_target_pairs={{0,1},{1,2},{2,3},{3,0},{4,5},{5,6},{6,7},{7,4},{8,9},{9,10},{10,1... | collective-permute-start | bytes 1204232 | tf_op jit(solution)/shard_map/ppermute | solution.py:379
  15.6 0.7 collective-permute-start.2
  16.3 2.1 %collective-permute-start.3 = (f32[16,6272]{1,0:T(8,128)S(1)}, f32[16,6272]{1,0:T(8,128)S(1)}, u32[]{:S(2)}, u32[]{:S(2)}) collective-permute-start(f32[16,6272]{1,0:T(8,128)S(1)} %pad_maximum_fusion.3), channel_id=1, source_target_pairs={{0,3},{1,0},{2,1},{3,2},{4,7},{5,4},{6,5},{7,6},{8,11},{9,8},{10,9... | collective-permute-start | bytes 1204232 | tf_op jit(solution)/shard_map/ppermute | solution.py:379
  18.4 0.8 pad_maximum_fusion.p0_ref
  19.1 0.4 collective-permute-done.4.p1_ref
  19.6 10.5 %gram_first.1 = (f32[64,2176]{1,0:T(8,128)S(1)}, f32[1024,1024]{1,0:T(8,128)S(1)}, f32[4,256,256]{2,1,0:T(8,128)S(1)}) custom-call(s32[2]{0:T(128)S(1)} %pad_add_fusion.1.place_ref, f32[16,2176]{1,0:T(8,128)S(1)} %get-tuple-element.24.p0_ref, f32[16,2176]{1,0:T(8,128)S(1)} %collective-permute-done.4.p1_ref, f32[16,2176]{1,0:T(8,128)S(1)} %collective-permute-done.5.p2_ref, ...), custom_call_target="tpu_custom_call" | custom-call | tf_op jit(solution)/shard_map/gram_first/pallas_call | solution.py:167
  30.1 6.7 %collective-permute-done.1.p1_ref = f32[16,6272]{1,0:T(8,128)S(1)} collective-permute-done((f32[16,6272]{1,0:T(8,128)S(1)}, f32[16,6272]{1,0:T(8,128)S(1)}, u32[]{:S(2)}, u32[]{:S(2)}) %collective-permute-start.1) | collective-permute-done | bytes 401440 | tf_op jit(solution)/shard_map/ppermute | solution.py:379
  36.8 0.7 copy-done
  37.8 26.6 %gram_last.1 = (f32[64,8320]{1,0:T(8,128)S(1)}, f32[64,40,128]{2,1,0:T(8,128)S(1)}, f32[64,40,128]{2,1,0:T(8,128)S(1)}) custom-call(s32[2]{0:T(128)S(1)} %pad_add_fusion.1.place_ref, f32[16,6272]{1,0:T(8,128)} %pad_maximum_fusion.p0_ref, f32[16,6272]{1,0:T(8,128)} %copy-done, f32[16,6272]{1,0:T(8,128)} %copy-done.1, f32[16,6272]{1,0:T(8,128)} %copy-done.2, ...), custom_call_target="tpu_custom_call" | custom-call | tf_op jit(solution)/shard_map/gram_last/pallas_call | solution.py:167
  64.5 0.6 collective-permute-start.7
  65.0 2.7 %collective-permute-done.7 = f32[64,40,128]{2,1,0:T(8,128)S(1)} collective-permute-done((f32[64,40,128]{2,1,0:T(8,128)S(1)}, f32[64,40,128]{2,1,0:T(8,128)S(1)}, u32[]{:S(2)}, u32[]{:S(2)}) %collective-permute-start.7) | collective-permute-done | bytes 1310752 | tf_op jit(solution)/shard_map/ppermute | solution.py:397
  67.8 27.4 %all_to_all.10 = f32[64,40,128]{2,1,0:T(8,128)S(1)} all-to-all(f32[64,40,128]{2,1,0:T(8,128)S(1)} %add.139), channel_id=1, replica_groups=mesh['x'=4,'y'=4,'core'=2,'chan'=4] {'x','y','chan'}, dimensions={0} | all-to-all | bytes 2621440 | tf_op jit(solution)/shard_map/all_to_all | solution.py:398
  95.5 24.2 %all_to_all.11.own_ref = f32[64,40,128]{2,1,0:T(8,128)S(1)} all-to-all(f32[64,40,128]{2,1,0:T(8,128)S(1)} %broadcast_in_dim.2), channel_id=1, replica_groups=mesh['x'=4,'y'=4,'core'=2,'chan'=4] {'x','y','chan'}, dimensions={0} | all-to-all | bytes 2621440 | tf_op jit(solution)/shard_map/all_to_all | solution.py:400
  119.7 3.6 %collective-permute-start.8 = (f32[64,40,128]{2,1,0:T(8,128)S(1)}, f32[64,40,128]{2,1,0:T(8,128)}, u32[]{:S(2)}, u32[]{:S(2)}) collective-permute-start(f32[64,40,128]{2,1,0:T(8,128)S(1)} %all_to_all.11.own_ref), channel_id=1, source_target_pairs={{0,4},{4,0},{1,5},{5,1},{2,6},{6,2},{3,7},{7,3},{8,12},{12,8},{9,1... | collective-permute-start | bytes 3932168 | tf_op jit(solution)/shard_map/ppermute | solution.py:401
  123.4 2.7 %collective-permute-done.8.other_ref = f32[64,40,128]{2,1,0:T(8,128)} collective-permute-done((f32[64,40,128]{2,1,0:T(8,128)S(1)}, f32[64,40,128]{2,1,0:T(8,128)}, u32[]{:S(2)}, u32[]{:S(2)}) %collective-permute-start.8) | collective-permute-done | bytes 1310752 | tf_op jit(solution)/shard_map/ppermute | solution.py:401
  126.1 40.3 %factor.1 = (f32[8,1024]{1,0:T(8,128)}, f32[128,512]{1,0:T(8,128)S(1)}) custom-call(s32[2]{0:T(128)S(1)} %pad_add_fusion.place_ref, f32[64,40,128]{2,1,0:T(8,128)S(1)} %all_to_all.11.own_ref, f32[64,40,128]{2,1,0:T(8,128)} %collective-permute-done.8.other_ref, f32[512,128]{1,0:T(8,128)} %given_ref.1), custom_call_target="tpu_custom_call" | custom-call | tf_op jit(solution)/shard_map/factor/pallas_call | solution.py:305
  166.4 7.6 %states.1 = f32[128,8192]{1,0:T(8,128)} custom-call(f32[128,512]{1,0:T(8,128)S(1)} %get-tuple-element.16.basis_ref, f32[64,8320]{1,0:T(8,128)S(1)} %get-tuple-element.17.x_ref), custom_call_target="tpu_custom_call" | custom-call | tf_op jit(solution)/shard_map/states/pallas_call | solution.py:346
  (19 shorter events, 0.9 us)
Async XLA Ops:
  1.3 11.3 %collective-permute-start = (f32[16,128]{1,0:T(8,128)S(1)}, f32[16,128]{1,0:T(8,128)S(1)}, u32[]{:S(2)}, u32[]{:S(2)}) collective-permute-start(f32[16,128]{1,0:T(8,128)S(1)} %slice.3), channel_id=1, source_target_pairs={{4,0},{8,4},{12,8},{16,12},{20,16},{24,20},{28,24},{32,28},{36,32}... | collective-permute-start | bytes 24584 | tf_op jit(solution)/shard_map/ppermute | solution.py:389
  5.9 10.4 %collective-permute-start.6 = (f32[16,2176]{1,0:T(8,128)S(1)}, f32[16,2176]{1,0:T(8,128)S(1)}, u32[]{:S(2)}, u32[]{:S(2)}) collective-permute-start(f32[16,2176]{1,0:T(8,128)S(1)} %get-tuple-element.22), channel_id=1, source_target_pairs={{0,3},{1,0},{2,1},{3,2},{4,7},{5,4},{6,5},{7,6},{8,11},{9,8},{10,9... | collective-permute-start | bytes 417800 | tf_op jit(solution)/shard_map/ppermute | solution.py:379
  9.8 9.8 %collective-permute-start.4 = (f32[16,2176]{1,0:T(8,128)S(1)}, f32[16,2176]{1,0:T(8,128)S(1)}, u32[]{:S(2)}, u32[]{:S(2)}) collective-permute-start(f32[16,2176]{1,0:T(8,128)S(1)} %get-tuple-element.23), channel_id=1, source_target_pairs={{0,1},{1,2},{2,3},{3,0},{4,5},{5,6},{6,7},{7,4},{8,9},{9,10},{10,1... | collective-permute-start | bytes 417800 | tf_op jit(solution)/shard_map/ppermute | solution.py:379
  9.8 9.8 %collective-permute-start.5 = (f32[16,2176]{1,0:T(8,128)S(1)}, f32[16,2176]{1,0:T(8,128)S(1)}, u32[]{:S(2)}, u32[]{:S(2)}) collective-permute-start(f32[16,2176]{1,0:T(8,128)S(1)} %get-tuple-element.25), channel_id=1, source_target_pairs={{0,2},{1,3},{2,0},{3,1},{4,6},{5,7},{6,4},{7,5},{8,10},{9,11},{10,... | collective-permute-start | bytes 417800 | tf_op jit(solution)/shard_map/ppermute | solution.py:379
  13.5 23.2 %collective-permute-start.1 = (f32[16,6272]{1,0:T(8,128)S(1)}, f32[16,6272]{1,0:T(8,128)S(1)}, u32[]{:S(2)}, u32[]{:S(2)}) collective-permute-start(f32[16,6272]{1,0:T(8,128)S(1)} %pad_maximum_fusion.1), channel_id=1, source_target_pairs={{0,1},{1,2},{2,3},{3,0},{4,5},{5,6},{6,7},{7,4},{8,9},{9,10},{10,1... | collective-permute-start | bytes 1204232 | tf_op jit(solution)/shard_map/ppermute | solution.py:379
  15.6 21.2 %collective-permute-start.2 = (f32[16,6272]{1,0:T(8,128)S(1)}, f32[16,6272]{1,0:T(8,128)S(1)}, u32[]{:S(2)}, u32[]{:S(2)}) collective-permute-start(f32[16,6272]{1,0:T(8,128)S(1)} %pad_maximum_fusion.2), channel_id=1, source_target_pairs={{0,2},{1,3},{2,0},{3,1},{4,6},{5,7},{6,4},{7,5},{8,10},{9,11},{10,... | collective-permute-start | bytes 1204232 | tf_op jit(solution)/shard_map/ppermute | solution.py:379
  16.3 20.5 %collective-permute-start.3 = (f32[16,6272]{1,0:T(8,128)S(1)}, f32[16,6272]{1,0:T(8,128)S(1)}, u32[]{:S(2)}, u32[]{:S(2)}) collective-permute-start(f32[16,6272]{1,0:T(8,128)S(1)} %pad_maximum_fusion.3), channel_id=1, source_target_pairs={{0,3},{1,0},{2,1},{3,2},{4,7},{5,4},{6,5},{7,6},{8,11},{9,8},{10,9... | collective-permute-start | bytes 1204232 | tf_op jit(solution)/shard_map/ppermute | solution.py:379
  36.8 0.7 copy-start
  36.8 0.9 copy-start.1
  36.8 1.1 copy-start.2
  64.5 3.3 %collective-permute-start.7 = (f32[64,40,128]{2,1,0:T(8,128)S(1)}, f32[64,40,128]{2,1,0:T(8,128)S(1)}, u32[]{:S(2)}, u32[]{:S(2)}) collective-permute-start(f32[64,40,128]{2,1,0:T(8,128)S(1)} %get-tuple-element.14), channel_id=1, source_target_pairs={{0,4},{4,0},{1,5},{5,1},{2,6},{6,2},{3,7},{7,3},{8,12},{12,8},{9,1... | collective-permute-start | bytes 3932168 | tf_op jit(solution)/shard_map/ppermute | solution.py:397
  119.7 6.4 %collective-permute-start.8 = (f32[64,40,128]{2,1,0:T(8,128)S(1)}, f32[64,40,128]{2,1,0:T(8,128)}, u32[]{:S(2)}, u32[]{:S(2)}) collective-permute-start(f32[64,40,128]{2,1,0:T(8,128)S(1)} %all_to_all.11.own_ref), channel_id=1, source_target_pairs={{0,4},{4,0},{1,5},{5,1},{2,6},{6,2},{3,7},{7,3},{8,12},{12,8},{9,1... | collective-permute-start | bytes 3932168 | tf_op jit(solution)/shard_map/ppermute | solution.py:401

commit v7 on v6

--- a/solution.py
+++ b/solution.py
@@ -22,7 +22,6 @@
 TILES = 640
 F32 = jnp.float32
 BF16 = jnp.bfloat16
-EXACT = lax.Precision.HIGHEST
 ALL = ("x", "y", "core", "chan")
 TIME = ("x", "y", "core")
 CHIPS = ("x", "y", "chan")
@@ -42,6 +41,11 @@
     return lax.dot_general(
         left, right, dims, precision=precision, preferred_element_type=F32
     )
+
+
+def mul3(left, right, dims):
+    (lh, ll), (rh, rl) = split(left), split(right)
+    return mul(lh, rh, dims) + mul(lh, rl, dims) + mul(ll, rh, dims)
 
 
 def upper_tiles():
@@ -260,7 +264,7 @@
         @pl.when(p == q)
         def _():
             top, s = q * PANEL, (q + 1) * PANEL
-            panel = mul(inverse_ref[...], a[top:s, s:], NN, EXACT)
+            panel = mul3(inverse_ref[...], a[top:s, s:], NN)
             u[top:s, s:] = panel
             high, low = split(panel)
             for b in range(s, ORDER, BLOCK):
@@ -280,9 +284,9 @@
             s = (q + 1) * PANEL
             u[s:, q * PANEL : s] = jnp.zeros((ORDER - s, PANEL), F32)
         fetch.wait()
-        lead = mul(start_ref[...], u[HALF:, HALF:], TN, EXACT)
+        lead = mul3(start_ref[...], u[HALF:, HALF:], TN)
         basis = lead / jnp.sqrt(jnp.sum(lead * lead))
-        inner = mul(basis, basis, NT, EXACT)
+        inner = mul3(basis, basis, NT)
         states = inner.shape[0]
         eye = jnp.where(
             lax.broadcasted_iota(jnp.int32, (states, states), 0)
@@ -293,10 +297,10 @@
         total = None
         for step in range(NSTEPS):
             m = eye - 0.5 * inner
-            total = m if total is None else mul(total, m, NN, EXACT)
+            total = m if total is None else mul3(total, m, NN)
             if step < NSTEPS - 1:
-                inner = mul(mul(inner, m, NN, EXACT), m, NN, EXACT)
-        basis_ref[...] = mul(total, basis, NN, EXACT)
+                inner = mul3(mul3(inner, m, NN), m, NN)
+        basis_ref[...] = mul3(total, basis, NN)
 
 
 def factor_and_basis(place, own, other, start, share):
@@ -341,7 +345,7 @@
 def project(basis, x):
     states = basis.shape[0]
     count = x.shape[1] - PAD
-    span = 2048
+    span = 4096
     slab = pltpu.VMEM((HALF, span), BF16)
     return pl.pallas_call(
         states_kernel,

time: 174 us -> 173 us (level)
  Pallas kernels: 85 us -> 83 us
    pallas_call x1, Pallas kernels: 40.3 us -> 38.5 us  [factor_and_basis(): pl.pallas_call(factor_kernel, grid=(ORDER // PANEL,), out_shape=(jax.Shap...]
where the time goes in v7:
time: 173 us; the launch traced here: 172 us
  Pallas kernels  83 us (48%)
  blocking collectives  51.9 us (30%)
  starting transfers between devices  17.4 us (10%)
  waiting for transfers between devices  12.5 us (7%)
  local copies, waits for them, and re-layouts  4.46 us (3%)
  other arithmetic  2.11 us (1%)
    all_to_all x2, blocking collectives, per_device(): half = lax.all_to_all(half, CHIPS, 0, 0, tiled=True)  51.9 us
    pallas_call x1, Pallas kernels, factor_and_basis(): pl.pallas_call(factor_kernel, grid=(ORDER // PANEL,), out_shape=(jax.Shap...  38.5 us
    pallas_call x2, Pallas kernels, gram_chunk(): pl.pallas_call(functools.partial(gram_kernel, size, start), out_shape=(x,...  37.1 us
    ppermute x6, starting transfers between devices, exchange(): lax.ppermute(window, 'chan', [(i, (i + away) % chans) for i in range(chan...  9.97 us
    pallas_call x1, Pallas kernels, project(): pl.pallas_call(states_kernel, grid=(count // span,), out_shape=jax.ShapeD...  7.39 us
    ppermute x6, waiting for transfers between devices, exchange(): lax.ppermute(window, 'chan', [(i, (i + away) % chans) for i in range(chan...  7.08 us
    ppermute x1, starting transfers between devices, per_device(): other = lax.ppermute(half, 'core', swap)  3.56 us
  transfers between devices with their start and end apart: 9, of which 4 were waited for; matrix products, arithmetic and copies ran while one was open for 3% of the time, Pallas kernels for 6%

profile of v7, /device:TPU:1, one launch (start us, length us, event | category | flops | bytes accessed | tf_op | source)
XLA Modules:
  0.0 172.2 jit_solution(2345377562867816466)
XLA Ops:
  0.6 0.7 slice.3
  1.3 3.3 %collective-permute-start = (f32[16,128]{1,0:T(8,128)S(1)}, f32[16,128]{1,0:T(8,128)S(1)}, u32[]{:S(2)}, u32[]{:S(2)}) collective-permute-start(f32[16,128]{1,0:T(8,128)S(1)} %slice.3), channel_id=1, source_target_pairs={{4,0},{8,4},{12,8},{16,12},{20,16},{24,20},{28,24},{32,28},{36,32}... | collective-permute-start | bytes 24584 | tf_op jit(solution)/shard_map/ppermute | solution.py:393
  4.7 1.2 constant_dynamic-slice_fusion
  5.9 3.9 %collective-permute-start.6 = (f32[16,2176]{1,0:T(8,128)S(1)}, f32[16,2176]{1,0:T(8,128)S(1)}, u32[]{:S(2)}, u32[]{:S(2)}) collective-permute-start(f32[16,2176]{1,0:T(8,128)S(1)} %get-tuple-element.22), channel_id=1, source_target_pairs={{0,3},{1,0},{2,1},{3,2},{4,7},{5,4},{6,5},{7,6},{8,11},{9,8},{10,9... | collective-permute-start | bytes 417800 | tf_op jit(solution)/shard_map/ppermute | solution.py:383
  9.8 1.3 collective-permute-start.5
  11.1 1.5 constant_dynamic-slice_fusion.4
  12.6 0.9 dynamic-slice_select_fusion
  13.5 2.0 %collective-permute-start.1 = (f32[16,6272]{1,0:T(8,128)S(1)}, f32[16,6272]{1,0:T(8,128)S(1)}, u32[]{:S(2)}, u32[]{:S(2)}) collective-permute-start(f32[16,6272]{1,0:T(8,128)S(1)} %pad_maximum_fusion.1), channel_id=1, source_target_pairs={{0,1},{1,2},{2,3},{3,0},{4,5},{5,6},{6,7},{7,4},{8,9},{9,10},{10,1... | collective-permute-start | bytes 1204232 | tf_op jit(solution)/shard_map/ppermute | solution.py:383
  15.6 0.7 collective-permute-start.2
  16.3 2.1 %collective-permute-start.3 = (f32[16,6272]{1,0:T(8,128)S(1)}, f32[16,6272]{1,0:T(8,128)S(1)}, u32[]{:S(2)}, u32[]{:S(2)}) collective-permute-start(f32[16,6272]{1,0:T(8,128)S(1)} %pad_maximum_fusion.3), channel_id=1, source_target_pairs={{0,3},{1,0},{2,1},{3,2},{4,7},{5,4},{6,5},{7,6},{8,11},{9,8},{10,9... | collective-permute-start | bytes 1204232 | tf_op jit(solution)/shard_map/ppermute | solution.py:383
  18.4 0.8 pad_maximum_fusion.p0_ref
  19.1 0.4 collective-permute-done.4.p1_ref
  19.6 10.5 %gram_first.1 = (f32[64,2176]{1,0:T(8,128)S(1)}, f32[1024,1024]{1,0:T(8,128)S(1)}, f32[4,256,256]{2,1,0:T(8,128)S(1)}) custom-call(s32[2]{0:T(128)S(1)} %pad_add_fusion.1.place_ref, f32[16,2176]{1,0:T(8,128)S(1)} %get-tuple-element.24.p0_ref, f32[16,2176]{1,0:T(8,128)S(1)} %collective-permute-done.4.p1_ref, f32[16,2176]{1,0:T(8,128)S(1)} %collective-permute-done.5.p2_ref, ...), custom_call_target="tpu_custom_call" | custom-call | tf_op jit(solution)/shard_map/gram_first/pallas_call | solution.py:171
  30.1 6.7 %collective-permute-done.1.p1_ref = f32[16,6272]{1,0:T(8,128)S(1)} collective-permute-done((f32[16,6272]{1,0:T(8,128)S(1)}, f32[16,6272]{1,0:T(8,128)S(1)}, u32[]{:S(2)}, u32[]{:S(2)}) %collective-permute-start.1) | collective-permute-done | bytes 401440 | tf_op jit(solution)/shard_map/ppermute | solution.py:383
  36.8 0.7 copy-done
  37.8 26.6 %gram_last.1 = (f32[64,8320]{1,0:T(8,128)S(1)}, f32[64,40,128]{2,1,0:T(8,128)S(1)}, f32[64,40,128]{2,1,0:T(8,128)S(1)}) custom-call(s32[2]{0:T(128)S(1)} %pad_add_fusion.1.place_ref, f32[16,6272]{1,0:T(8,128)} %pad_maximum_fusion.p0_ref, f32[16,6272]{1,0:T(8,128)} %copy-done, f32[16,6272]{1,0:T(8,128)} %copy-done.1, f32[16,6272]{1,0:T(8,128)} %copy-done.2, ...), custom_call_target="tpu_custom_call" | custom-call | tf_op jit(solution)/shard_map/gram_last/pallas_call | solution.py:171
  64.5 0.6 collective-permute-start.7
  65.0 2.7 %collective-permute-done.7 = f32[64,40,128]{2,1,0:T(8,128)S(1)} collective-permute-done((f32[64,40,128]{2,1,0:T(8,128)S(1)}, f32[64,40,128]{2,1,0:T(8,128)S(1)}, u32[]{:S(2)}, u32[]{:S(2)}) %collective-permute-start.7) | collective-permute-done | bytes 1310752 | tf_op jit(solution)/shard_map/ppermute | solution.py:401
  67.8 27.7 %all_to_all.10 = f32[64,40,128]{2,1,0:T(8,128)S(1)} all-to-all(f32[64,40,128]{2,1,0:T(8,128)S(1)} %add.139), channel_id=1, replica_groups=mesh['x'=4,'y'=4,'core'=2,'chan'=4] {'x','y','chan'}, dimensions={0} | all-to-all | bytes 2621440 | tf_op jit(solution)/shard_map/all_to_all | solution.py:402
  95.7 24.2 %all_to_all.11.own_ref = f32[64,40,128]{2,1,0:T(8,128)S(1)} all-to-all(f32[64,40,128]{2,1,0:T(8,128)S(1)} %broadcast_in_dim.2), channel_id=1, replica_groups=mesh['x'=4,'y'=4,'core'=2,'chan'=4] {'x','y','chan'}, dimensions={0} | all-to-all | bytes 2621440 | tf_op jit(solution)/shard_map/all_to_all | solution.py:404
  119.9 3.6 %collective-permute-start.8 = (f32[64,40,128]{2,1,0:T(8,128)S(1)}, f32[64,40,128]{2,1,0:T(8,128)}, u32[]{:S(2)}, u32[]{:S(2)}) collective-permute-start(f32[64,40,128]{2,1,0:T(8,128)S(1)} %all_to_all.11.own_ref), channel_id=1, source_target_pairs={{0,4},{4,0},{1,5},{5,1},{2,6},{6,2},{3,7},{7,3},{8,12},{12,8},{9,1... | collective-permute-start | bytes 3932168 | tf_op jit(solution)/shard_map/ppermute | solution.py:405
  123.6 2.7 %collective-permute-done.8.other_ref = f32[64,40,128]{2,1,0:T(8,128)} collective-permute-done((f32[64,40,128]{2,1,0:T(8,128)S(1)}, f32[64,40,128]{2,1,0:T(8,128)}, u32[]{:S(2)}, u32[]{:S(2)}) %collective-permute-start.8) | collective-permute-done | bytes 1310752 | tf_op jit(solution)/shard_map/ppermute | solution.py:405
  126.3 38.5 %factor.1 = (f32[8,1024]{1,0:T(8,128)}, f32[128,512]{1,0:T(8,128)S(1)}) custom-call(s32[2]{0:T(128)S(1)} %pad_add_fusion.place_ref, f32[64,40,128]{2,1,0:T(8,128)S(1)} %all_to_all.11.own_ref, f32[64,40,128]{2,1,0:T(8,128)} %collective-permute-done.8.other_ref, f32[512,128]{1,0:T(8,128)} %given_ref.1), custom_call_target="tpu_custom_call" | custom-call | tf_op jit(solution)/shard_map/factor/pallas_call | solution.py:309
  164.8 7.4 %states.1 = f32[128,8192]{1,0:T(8,128)} custom-call(f32[128,512]{1,0:T(8,128)S(1)} %get-tuple-element.16.basis_ref, f32[64,8320]{1,0:T(8,128)S(1)} %get-tuple-element.17.x_ref), custom_call_target="tpu_custom_call" | custom-call | tf_op jit(solution)/shard_map/states/pallas_call | solution.py:350
  (19 shorter events, 0.9 us)
Async XLA Ops:
  1.3 11.3 %collective-permute-start = (f32[16,128]{1,0:T(8,128)S(1)}, f32[16,128]{1,0:T(8,128)S(1)}, u32[]{:S(2)}, u32[]{:S(2)}) collective-permute-start(f32[16,128]{1,0:T(8,128)S(1)} %slice.3), channel_id=1, source_target_pairs={{4,0},{8,4},{12,8},{16,12},{20,16},{24,20},{28,24},{32,28},{36,32}... | collective-permute-start | bytes 24584 | tf_op jit(solution)/shard_map/ppermute | solution.py:393
  5.9 10.4 %collective-permute-start.6 = (f32[16,2176]{1,0:T(8,128)S(1)}, f32[16,2176]{1,0:T(8,128)S(1)}, u32[]{:S(2)}, u32[]{:S(2)}) collective-permute-start(f32[16,2176]{1,0:T(8,128)S(1)} %get-tuple-element.22), channel_id=1, source_target_pairs={{0,3},{1,0},{2,1},{3,2},{4,7},{5,4},{6,5},{7,6},{8,11},{9,8},{10,9... | collective-permute-start | bytes 417800 | tf_op jit(solution)/shard_map/ppermute | solution.py:383
  9.8 9.8 %collective-permute-start.4 = (f32[16,2176]{1,0:T(8,128)S(1)}, f32[16,2176]{1,0:T(8,128)S(1)}, u32[]{:S(2)}, u32[]{:S(2)}) collective-permute-start(f32[16,2176]{1,0:T(8,128)S(1)} %get-tuple-element.23), channel_id=1, source_target_pairs={{0,1},{1,2},{2,3},{3,0},{4,5},{5,6},{6,7},{7,4},{8,9},{9,10},{10,1... | collective-permute-start | bytes 417800 | tf_op jit(solution)/shard_map/ppermute | solution.py:383
  9.8 9.8 %collective-permute-start.5 = (f32[16,2176]{1,0:T(8,128)S(1)}, f32[16,2176]{1,0:T(8,128)S(1)}, u32[]{:S(2)}, u32[]{:S(2)}) collective-permute-start(f32[16,2176]{1,0:T(8,128)S(1)} %get-tuple-element.25), channel_id=1, source_target_pairs={{0,2},{1,3},{2,0},{3,1},{4,6},{5,7},{6,4},{7,5},{8,10},{9,11},{10,... | collective-permute-start | bytes 417800 | tf_op jit(solution)/shard_map/ppermute | solution.py:383
  13.5 23.2 %collective-permute-start.1 = (f32[16,6272]{1,0:T(8,128)S(1)}, f32[16,6272]{1,0:T(8,128)S(1)}, u32[]{:S(2)}, u32[]{:S(2)}) collective-permute-start(f32[16,6272]{1,0:T(8,128)S(1)} %pad_maximum_fusion.1), channel_id=1, source_target_pairs={{0,1},{1,2},{2,3},{3,0},{4,5},{5,6},{6,7},{7,4},{8,9},{9,10},{10,1... | collective-permute-start | bytes 1204232 | tf_op jit(solution)/shard_map/ppermute | solution.py:383
  15.6 21.2 %collective-permute-start.2 = (f32[16,6272]{1,0:T(8,128)S(1)}, f32[16,6272]{1,0:T(8,128)S(1)}, u32[]{:S(2)}, u32[]{:S(2)}) collective-permute-start(f32[16,6272]{1,0:T(8,128)S(1)} %pad_maximum_fusion.2), channel_id=1, source_target_pairs={{0,2},{1,3},{2,0},{3,1},{4,6},{5,7},{6,4},{7,5},{8,10},{9,11},{10,... | collective-permute-start | bytes 1204232 | tf_op jit(solution)/shard_map/ppermute | solution.py:383
  16.3 20.5 %collective-permute-start.3 = (f32[16,6272]{1,0:T(8,128)S(1)}, f32[16,6272]{1,0:T(8,128)S(1)}, u32[]{:S(2)}, u32[]{:S(2)}) collective-permute-start(f32[16,6272]{1,0:T(8,128)S(1)} %pad_maximum_fusion.3), channel_id=1, source_target_pairs={{0,3},{1,0},{2,1},{3,2},{4,7},{5,4},{6,5},{7,6},{8,11},{9,8},{10,9... | collective-permute-start | bytes 1204232 | tf_op jit(solution)/shard_map/ppermute | solution.py:383
  36.8 0.7 copy-start
  36.8 0.9 copy-start.1
  36.8 1.1 copy-start.2
  64.5 3.3 %collective-permute-start.7 = (f32[64,40,128]{2,1,0:T(8,128)S(1)}, f32[64,40,128]{2,1,0:T(8,128)S(1)}, u32[]{:S(2)}, u32[]{:S(2)}) collective-permute-start(f32[64,40,128]{2,1,0:T(8,128)S(1)} %get-tuple-element.14), channel_id=1, source_target_pairs={{0,4},{4,0},{1,5},{5,1},{2,6},{6,2},{3,7},{7,3},{8,12},{12,8},{9,1... | collective-permute-start | bytes 3932168 | tf_op jit(solution)/shard_map/ppermute | solution.py:401
  119.9 6.3 %collective-permute-start.8 = (f32[64,40,128]{2,1,0:T(8,128)S(1)}, f32[64,40,128]{2,1,0:T(8,128)}, u32[]{:S(2)}, u32[]{:S(2)}) collective-permute-start(f32[64,40,128]{2,1,0:T(8,128)S(1)} %all_to_all.11.own_ref), channel_id=1, source_target_pairs={{0,4},{4,0},{1,5},{5,1},{2,6},{6,2},{3,7},{7,3},{8,12},{12,8},{9,1... | collective-permute-start | bytes 3932168 | tf_op jit(solution)/shard_map/ppermute | solution.py:405

commit v8 on v7

--- a/solution.py
+++ b/solution.py
@@ -24,7 +24,7 @@
 BF16 = jnp.bfloat16
 ALL = ("x", "y", "core", "chan")
 TIME = ("x", "y", "core")
-CHIPS = ("x", "y", "chan")
+CHIPS = ("y", "chan", "x")
 NN = (((1,), (0,)), ((), ()))
 NT = (((1,), (1,)), ((), ()))
 TN = (((0,), (0,)), ((), ()))

time: 173 us -> 173 us (level)
  no operation moved by 1% of the time
where the time goes in v8:
time: 173 us; the launch traced here: 172 us
  Pallas kernels  83 us (48%)
  blocking collectives  52.6 us (30%)
  starting transfers between devices  17 us (10%)
  waiting for transfers between devices  12.5 us (7%)
  local copies, waits for them, and re-layouts  4.46 us (3%)
  other arithmetic  2.11 us (1%)
    all_to_all x2, blocking collectives, per_device(): half = lax.all_to_all(half, CHIPS, 0, 0, tiled=True)  52.6 us
    pallas_call x1, Pallas kernels, factor_and_basis(): pl.pallas_call(factor_kernel, grid=(ORDER // PANEL,), out_shape=(jax.Shap...  38.5 us
    pallas_call x2, Pallas kernels, gram_chunk(): pl.pallas_call(functools.partial(gram_kernel, size, start), out_shape=(x,...  37.1 us
    ppermute x6, starting transfers between devices, exchange(): lax.ppermute(window, 'chan', [(i, (i + away) % chans) for i in range(chan...  9.97 us
    pallas_call x1, Pallas kernels, project(): pl.pallas_call(states_kernel, grid=(count // span,), out_shape=jax.ShapeD...  7.39 us
    ppermute x6, waiting for transfers between devices, exchange(): lax.ppermute(window, 'chan', [(i, (i + away) % chans) for i in range(chan...  7.08 us
  transfers between devices with their start and end apart: 9, of which 4 were waited for; matrix products, arithmetic and copies ran while one was open for 3% of the time, Pallas kernels for 6%

profile of v8, /device:TPU:1, one launch (start us, length us, event | category | flops | bytes accessed | tf_op | source)
XLA Modules:
  0.0 172.4 jit_solution(11730220928034660465)
XLA Ops:
  0.6 0.7 slice.3
  1.3 3.3 %collective-permute-start = (f32[16,128]{1,0:T(8,128)S(1)}, f32[16,128]{1,0:T(8,128)S(1)}, u32[]{:S(2)}, u32[]{:S(2)}) collective-permute-start(f32[16,128]{1,0:T(8,128)S(1)} %slice.3), channel_id=1, source_target_pairs={{4,0},{8,4},{12,8},{16,12},{20,16},{24,20},{28,24},{32,28},{36,32}... | collective-permute-start | bytes 24584 | tf_op jit(solution)/shard_map/ppermute | solution.py:393
  4.7 1.2 constant_dynamic-slice_fusion
  5.9 3.9 %collective-permute-start.6 = (f32[16,2176]{1,0:T(8,128)S(1)}, f32[16,2176]{1,0:T(8,128)S(1)}, u32[]{:S(2)}, u32[]{:S(2)}) collective-permute-start(f32[16,2176]{1,0:T(8,128)S(1)} %get-tuple-element.22), channel_id=1, source_target_pairs={{0,3},{1,0},{2,1},{3,2},{4,7},{5,4},{6,5},{7,6},{8,11},{9,8},{10,9... | collective-permute-start | bytes 417800 | tf_op jit(solution)/shard_map/ppermute | solution.py:383
  9.8 1.3 collective-permute-start.5
  11.1 1.5 constant_dynamic-slice_fusion.4
  12.6 0.9 dynamic-slice_select_fusion
  13.5 2.0 %collective-permute-start.1 = (f32[16,6272]{1,0:T(8,128)S(1)}, f32[16,6272]{1,0:T(8,128)S(1)}, u32[]{:S(2)}, u32[]{:S(2)}) collective-permute-start(f32[16,6272]{1,0:T(8,128)S(1)} %pad_maximum_fusion.1), channel_id=1, source_target_pairs={{0,1},{1,2},{2,3},{3,0},{4,5},{5,6},{6,7},{7,4},{8,9},{9,10},{10,1... | collective-permute-start | bytes 1204232 | tf_op jit(solution)/shard_map/ppermute | solution.py:383
  15.6 0.7 collective-permute-start.2
  16.3 2.1 %collective-permute-start.3 = (f32[16,6272]{1,0:T(8,128)S(1)}, f32[16,6272]{1,0:T(8,128)S(1)}, u32[]{:S(2)}, u32[]{:S(2)}) collective-permute-start(f32[16,6272]{1,0:T(8,128)S(1)} %pad_maximum_fusion.3), channel_id=1, source_target_pairs={{0,3},{1,0},{2,1},{3,2},{4,7},{5,4},{6,5},{7,6},{8,11},{9,8},{10,9... | collective-permute-start | bytes 1204232 | tf_op jit(solution)/shard_map/ppermute | solution.py:383
  18.4 0.8 pad_maximum_fusion.p0_ref
  19.1 0.4 collective-permute-done.4.p1_ref
  19.6 10.5 %gram_first.1 = (f32[64,2176]{1,0:T(8,128)S(1)}, f32[1024,1024]{1,0:T(8,128)S(1)}, f32[4,256,256]{2,1,0:T(8,128)S(1)}) custom-call(s32[2]{0:T(128)S(1)} %pad_add_fusion.1.place_ref, f32[16,2176]{1,0:T(8,128)S(1)} %get-tuple-element.24.p0_ref, f32[16,2176]{1,0:T(8,128)S(1)} %collective-permute-done.4.p1_ref, f32[16,2176]{1,0:T(8,128)S(1)} %collective-permute-done.5.p2_ref, ...), custom_call_target="tpu_custom_call" | custom-call | tf_op jit(solution)/shard_map/gram_first/pallas_call | solution.py:171
  30.1 6.7 %collective-permute-done.1.p1_ref = f32[16,6272]{1,0:T(8,128)S(1)} collective-permute-done((f32[16,6272]{1,0:T(8,128)S(1)}, f32[16,6272]{1,0:T(8,128)S(1)}, u32[]{:S(2)}, u32[]{:S(2)}) %collective-permute-start.1) | collective-permute-done | bytes 401440 | tf_op jit(solution)/shard_map/ppermute | solution.py:383
  36.8 0.7 copy-done
  37.8 26.6 %gram_last.1 = (f32[64,8320]{1,0:T(8,128)S(1)}, f32[64,40,128]{2,1,0:T(8,128)S(1)}, f32[64,40,128]{2,1,0:T(8,128)S(1)}) custom-call(s32[2]{0:T(128)S(1)} %pad_add_fusion.1.place_ref, f32[16,6272]{1,0:T(8,128)} %pad_maximum_fusion.p0_ref, f32[16,6272]{1,0:T(8,128)} %copy-done, f32[16,6272]{1,0:T(8,128)} %copy-done.1, f32[16,6272]{1,0:T(8,128)} %copy-done.2, ...), custom_call_target="tpu_custom_call" | custom-call | tf_op jit(solution)/shard_map/gram_last/pallas_call | solution.py:171
  64.5 0.6 collective-permute-start.7
  65.0 2.7 %collective-permute-done.7 = f32[64,40,128]{2,1,0:T(8,128)S(1)} collective-permute-done((f32[64,40,128]{2,1,0:T(8,128)S(1)}, f32[64,40,128]{2,1,0:T(8,128)S(1)}, u32[]{:S(2)}, u32[]{:S(2)}) %collective-permute-start.7) | collective-permute-done | bytes 1310752 | tf_op jit(solution)/shard_map/ppermute | solution.py:401
  67.8 28.9 %all_to_all.10 = f32[64,40,128]{2,1,0:T(8,128)S(1)} all-to-all(f32[64,40,128]{2,1,0:T(8,128)S(1)} %add.139), channel_id=1, replica_groups=mesh['x'=4,'y'=4,'core'=2,'chan'=4] {'y','chan','x'}, dimensions={0} | all-to-all | bytes 2621440 | tf_op jit(solution)/shard_map/all_to_all | solution.py:402
  96.9 23.7 %all_to_all.11.own_ref = f32[64,40,128]{2,1,0:T(8,128)S(1)} all-to-all(f32[64,40,128]{2,1,0:T(8,128)S(1)} %broadcast_in_dim.2), channel_id=1, replica_groups=mesh['x'=4,'y'=4,'core'=2,'chan'=4] {'y','chan','x'}, dimensions={0} | all-to-all | bytes 2621440 | tf_op jit(solution)/shard_map/all_to_all | solution.py:404
  120.6 3.1 %collective-permute-start.8 = (f32[64,40,128]{2,1,0:T(8,128)S(1)}, f32[64,40,128]{2,1,0:T(8,128)}, u32[]{:S(2)}, u32[]{:S(2)}) collective-permute-start(f32[64,40,128]{2,1,0:T(8,128)S(1)} %all_to_all.11.own_ref), channel_id=1, source_target_pairs={{0,4},{4,0},{1,5},{5,1},{2,6},{6,2},{3,7},{7,3},{8,12},{12,8},{9,1... | collective-permute-start | bytes 3932168 | tf_op jit(solution)/shard_map/ppermute | solution.py:405
  123.8 2.7 %collective-permute-done.8.other_ref = f32[64,40,128]{2,1,0:T(8,128)} collective-permute-done((f32[64,40,128]{2,1,0:T(8,128)S(1)}, f32[64,40,128]{2,1,0:T(8,128)}, u32[]{:S(2)}, u32[]{:S(2)}) %collective-permute-start.8) | collective-permute-done | bytes 1310752 | tf_op jit(solution)/shard_map/ppermute | solution.py:405
  126.5 38.5 %factor.1 = (f32[8,1024]{1,0:T(8,128)}, f32[128,512]{1,0:T(8,128)S(1)}) custom-call(s32[2]{0:T(128)S(1)} %pad_add_fusion.place_ref, f32[64,40,128]{2,1,0:T(8,128)S(1)} %all_to_all.11.own_ref, f32[64,40,128]{2,1,0:T(8,128)} %collective-permute-done.8.other_ref, f32[512,128]{1,0:T(8,128)} %given_ref.1), custom_call_target="tpu_custom_call" | custom-call | tf_op jit(solution)/shard_map/factor/pallas_call | solution.py:309
  165.0 7.4 %states.1 = f32[128,8192]{1,0:T(8,128)} custom-call(f32[128,512]{1,0:T(8,128)S(1)} %get-tuple-element.16.basis_ref, f32[64,8320]{1,0:T(8,128)S(1)} %get-tuple-element.17.x_ref), custom_call_target="tpu_custom_call" | custom-call | tf_op jit(solution)/shard_map/states/pallas_call | solution.py:350
  (19 shorter events, 0.9 us)
Async XLA Ops:
  1.3 11.3 %collective-permute-start = (f32[16,128]{1,0:T(8,128)S(1)}, f32[16,128]{1,0:T(8,128)S(1)}, u32[]{:S(2)}, u32[]{:S(2)}) collective-permute-start(f32[16,128]{1,0:T(8,128)S(1)} %slice.3), channel_id=1, source_target_pairs={{4,0},{8,4},{12,8},{16,12},{20,16},{24,20},{28,24},{32,28},{36,32}... | collective-permute-start | bytes 24584 | tf_op jit(solution)/shard_map/ppermute | solution.py:393
  5.9 10.4 %collective-permute-start.6 = (f32[16,2176]{1,0:T(8,128)S(1)}, f32[16,2176]{1,0:T(8,128)S(1)}, u32[]{:S(2)}, u32[]{:S(2)}) collective-permute-start(f32[16,2176]{1,0:T(8,128)S(1)} %get-tuple-element.22), channel_id=1, source_target_pairs={{0,3},{1,0},{2,1},{3,2},{4,7},{5,4},{6,5},{7,6},{8,11},{9,8},{10,9... | collective-permute-start | bytes 417800 | tf_op jit(solution)/shard_map/ppermute | solution.py:383
  9.8 9.8 %collective-permute-start.4 = (f32[16,2176]{1,0:T(8,128)S(1)}, f32[16,2176]{1,0:T(8,128)S(1)}, u32[]{:S(2)}, u32[]{:S(2)}) collective-permute-start(f32[16,2176]{1,0:T(8,128)S(1)} %get-tuple-element.23), channel_id=1, source_target_pairs={{0,1},{1,2},{2,3},{3,0},{4,5},{5,6},{6,7},{7,4},{8,9},{9,10},{10,1... | collective-permute-start | bytes 417800 | tf_op jit(solution)/shard_map/ppermute | solution.py:383
  9.8 9.8 %collective-permute-start.5 = (f32[16,2176]{1,0:T(8,128)S(1)}, f32[16,2176]{1,0:T(8,128)S(1)}, u32[]{:S(2)}, u32[]{:S(2)}) collective-permute-start(f32[16,2176]{1,0:T(8,128)S(1)} %get-tuple-element.25), channel_id=1, source_target_pairs={{0,2},{1,3},{2,0},{3,1},{4,6},{5,7},{6,4},{7,5},{8,10},{9,11},{10,... | collective-permute-start | bytes 417800 | tf_op jit(solution)/shard_map/ppermute | solution.py:383
  13.5 23.2 %collective-permute-start.1 = (f32[16,6272]{1,0:T(8,128)S(1)}, f32[16,6272]{1,0:T(8,128)S(1)}, u32[]{:S(2)}, u32[]{:S(2)}) collective-permute-start(f32[16,6272]{1,0:T(8,128)S(1)} %pad_maximum_fusion.1), channel_id=1, source_target_pairs={{0,1},{1,2},{2,3},{3,0},{4,5},{5,6},{6,7},{7,4},{8,9},{9,10},{10,1... | collective-permute-start | bytes 1204232 | tf_op jit(solution)/shard_map/ppermute | solution.py:383
  15.6 21.2 %collective-permute-start.2 = (f32[16,6272]{1,0:T(8,128)S(1)}, f32[16,6272]{1,0:T(8,128)S(1)}, u32[]{:S(2)}, u32[]{:S(2)}) collective-permute-start(f32[16,6272]{1,0:T(8,128)S(1)} %pad_maximum_fusion.2), channel_id=1, source_target_pairs={{0,2},{1,3},{2,0},{3,1},{4,6},{5,7},{6,4},{7,5},{8,10},{9,11},{10,... | collective-permute-start | bytes 1204232 | tf_op jit(solution)/shard_map/ppermute | solution.py:383
  16.3 20.5 %collective-permute-start.3 = (f32[16,6272]{1,0:T(8,128)S(1)}, f32[16,6272]{1,0:T(8,128)S(1)}, u32[]{:S(2)}, u32[]{:S(2)}) collective-permute-start(f32[16,6272]{1,0:T(8,128)S(1)} %pad_maximum_fusion.3), channel_id=1, source_target_pairs={{0,3},{1,0},{2,1},{3,2},{4,7},{5,4},{6,5},{7,6},{8,11},{9,8},{10,9... | collective-permute-start | bytes 1204232 | tf_op jit(solution)/shard_map/ppermute | solution.py:383
  36.8 0.7 copy-start
  36.8 0.9 copy-start.1
  36.8 1.1 copy-start.2
  64.5 3.3 %collective-permute-start.7 = (f32[64,40,128]{2,1,0:T(8,128)S(1)}, f32[64,40,128]{2,1,0:T(8,128)S(1)}, u32[]{:S(2)}, u32[]{:S(2)}) collective-permute-start(f32[64,40,128]{2,1,0:T(8,128)S(1)} %get-tuple-element.14), channel_id=1, source_target_pairs={{0,4},{4,0},{1,5},{5,1},{2,6},{6,2},{3,7},{7,3},{8,12},{12,8},{9,1... | collective-permute-start | bytes 3932168 | tf_op jit(solution)/shard_map/ppermute | solution.py:401
  120.6 5.9 %collective-permute-start.8 = (f32[64,40,128]{2,1,0:T(8,128)S(1)}, f32[64,40,128]{2,1,0:T(8,128)}, u32[]{:S(2)}, u32[]{:S(2)}) collective-permute-start(f32[64,40,128]{2,1,0:T(8,128)S(1)} %all_to_all.11.own_ref), channel_id=1, source_target_pairs={{0,4},{4,0},{1,5},{5,1},{2,6},{6,2},{3,7},{7,3},{8,12},{12,8},{9,1... | collective-permute-start | bytes 3932168 | tf_op jit(solution)/shard_map/ppermute | solution.py:405
